TPU v7x, 32 devices: a whole 2x2x4 slice. The times are simulated.
32 devices in a mesh: tm: 16 (over z, x, core), rows: 2 (over y).
Axes of the slice: x: 2, y: 2, z: 4, core: 2. Of those that a mesh axis runs over, the one named last changes fastest.
Arguments:
- frames: bfloat16 [32, 16, 128, 128], P('tm', 'rows'), may hold values from -6 to 6
- conv_fine: bfloat16 [3, 3, 384, 128], replicated, may hold values from -0.109375 to 0.109375
- conv_down: bfloat16 [3, 384, 256], replicated, may hold values from -0.1875 to 0.1875
- conv_coarse: bfloat16 [3, 3, 768, 256], replicated, may hold values from -0.078125 to 0.078125
Outputs:
- coarse_out: bfloat16 [16, 8, 64, 256], P('tm', 'rows')
All inputs are finite; a program needn't handle non-finite values.
Results may differ from a plain program's by a relative error of at most 0.014.
Values may be sent and summed in bfloat16 or wider, within the bound.
No kernel may reach another device: no remote copies, remote signals or barrier semaphores. Data moves between devices by JAX's collectives and lax.ppermute only.
A program may use at most 64 MiB of HBM per device.

v0:
```python
import jax
import jax.numpy as jnp
from jax import lax
from jax.sharding import PartitionSpec as P


def shifted(value, axis, steps):
    count = lax.axis_size(axis)
    first, last = (max(0, -steps), min(count, count - steps))
    return lax.ppermute(value, axis, [(source, source + steps) for source in range(first, last)])


def padded_2(cells, sides, width):
    for axis, dim in sides:
        count = lax.axis_size(axis)
        ends = count - 1
        head = lax.slice_in_dim(cells, 0, width, axis=dim)
        tail = lax.slice_in_dim(cells, cells.shape[dim] - width, cells.shape[dim], axis=dim)
        cells = jnp.concatenate(
            [
                lax.ppermute(tail, axis, [(i, (i + 1) % count) for i in range(ends)]),
                cells,
                lax.ppermute(head, axis, [((i + 1) % count, i) for i in range(ends)]),
            ],
            axis=dim,
        )
    return cells


def conv_block(extended, weight, frames_out, rows_out):
    col_count = extended.shape[2]
    channels = extended.shape[3]
    padded = jnp.pad(extended, ((0, 0), (0, 0), (1, 1), (0, 0)))
    stacked = jnp.concatenate(
        [
            padded[:, :, 0:col_count],
            padded[:, :, 1 : col_count + 1],
            padded[:, :, 2 : col_count + 2],
        ],
        axis=3,
    )
    total = jnp.zeros((frames_out * rows_out * col_count, weight.shape[-1]), jnp.float32)
    for time_tap in range(3):
        for row_tap in range(3):
            window = stacked[
                time_tap : time_tap + frames_out, row_tap : row_tap + rows_out
            ].reshape(-1, 3 * channels)
            total = total + jnp.dot(
                window, weight[time_tap, row_tap], preferred_element_type=jnp.float32
            )
    return total


def local(frames, conv_fine, conv_down, conv_coarse):
    frame_count, rows_dev, col_count, channels = frames.shape
    earlier = shifted(frames, "tm", 1)
    joined = jnp.concatenate([earlier, frames], axis=0)
    extended = padded_2(joined, (("rows", 1),), 1)
    total = conv_block(extended, conv_fine, frame_count, rows_dev)
    fine_out = (
        jax.nn.silu(total).astype(jnp.bfloat16).reshape(frame_count, rows_dev, col_count, channels)
    )
    widened = fine_out.astype(jnp.float32)
    pooled = ((widened[0] + widened[1]) * 0.5).astype(jnp.bfloat16)
    edge_row = shifted(pooled[0:1], "rows", -1)
    with_rim = jnp.concatenate([pooled, edge_row], axis=0)
    with_rim = jnp.pad(with_rim, ((0, 0), (0, 1), (0, 0)))
    half_rows = rows_dev // 2
    half_cols = col_count // 2
    stacked = jnp.concatenate(
        [with_rim[:, col_tap : col_tap + col_count : 2] for col_tap in range(3)], axis=2
    )
    down_total = jnp.zeros((half_rows * half_cols, conv_down.shape[-1]), jnp.float32)
    for row_tap in range(3):
        window = stacked[row_tap : row_tap + rows_dev : 2].reshape(-1, 3 * channels)
        down_total = down_total + jnp.dot(
            window, conv_down[row_tap], preferred_element_type=jnp.float32
        )
    reduced = down_total.astype(jnp.bfloat16).reshape(1, half_rows, half_cols, -1)
    carried = reduced
    history = [reduced]
    for repeat in range(2):
        carried = shifted(carried, "tm", 1)
        history.insert(0, carried)
    coarse_joined = jnp.concatenate(history, axis=0)
    coarse_extended = padded_2(coarse_joined, (("rows", 1),), 1)
    coarse_total = conv_block(coarse_extended, conv_coarse, 1, half_rows)
    return jax.nn.silu(coarse_total).astype(jnp.bfloat16).reshape(1, half_rows, half_cols, -1)


def solution(mesh):
    placed = (P("tm", "rows", None, None), P(), P(), P())
    return jax.shard_map(
        local, mesh=mesh, in_specs=placed, out_specs=P("tm", "rows", None, None), check_vma=False
    )
```

profile of v0, /device:TPU:16, one launch (start us, length us, event | category | flops | bytes accessed | tf_op | source)
XLA Modules:
  0.0 70.2 jit_solution(408407516653237608)
XLA Ops:
  0.0 1.9 %collective-permute-start = (bf16[2,8,128,128]{3,2,1,0:T(8,128)(2,1)}, bf16[2,8,128,128]{3,2,1,0:T(8,128)(2,1)S(1)}, u32[]{:S(2)}, u32[]{:S(2)}) collective-permute-start(bf16[2,8,128,128]{3,2,1,0:T(8,128)(2,1)} %param.4), channel_id=1, source_target_pairs={{0,2},{2,4},{4,6},{6,8},{8,10},{10,12},{12,14},{14,16},{16,18},{18... | collective-permute-start | bytes 1572872 | tf_op jit(solution)/shard_map/ppermute | solution.py:10
  1.9 9.7 %collective-permute-done = bf16[2,8,128,128]{3,2,1,0:T(8,128)(2,1)S(1)} collective-permute-done((bf16[2,8,128,128]{3,2,1,0:T(8,128)(2,1)}, bf16[2,8,128,128]{3,2,1,0:T(8,128)(2,1)S(1)}, u32[]{:S(2)}, u32[]{:S(2)}) %collective-permute-start) | collective-permute-done | bytes 524320 | tf_op jit(solution)/shard_map/ppermute | solution.py:10
  11.6 1.1 %constant_dynamic-update-slice_fusion = bf16[4,8,128,128]{3,2,1,0:T(8,128)(2,1)S(1)} fusion(bf16[4,8,128,128]{3,2,1,0:T(8,128)(2,1)S(1)} %constant_dynamic-update-slice_fusion.1, bf16[2,8,128,128]{3,2,1,0:T(8,128)(2,1)} %param.4), kind=kLoop, calls=%fused_computation.113 | loop fusion | bytes 1048576 | tf_op jit(solution)/shard_map/concatenate | solution.py:57
  12.8 3.4 %collective-permute-start.1 = (bf16[4,1,128,128]{3,2,1,0:T(8,128)(2,1)S(1)}, bf16[4,1,128,128]{3,2,1,0:T(8,128)(2,1)S(1)}, u32[]{:S(2)}, u32[]{:S(2)}) collective-permute-start(bf16[4,1,128,128]{3,2,1,0:T(8,128)(2,1)S(1)} %get-tuple-element.25), channel_id=1, source_target_pairs={{0,1},{2,3},{4,5},{6,7},{8,9},{10,11},{12,13},{14,15},{16,17},{18,... | collective-permute-start | bytes 393224 | tf_op jit(solution)/shard_map/ppermute | solution.py:21
  16.2 1.3 %collective-permute-start.2 = (bf16[4,1,128,128]{3,2,1,0:T(8,128)(2,1)S(1)}, bf16[4,1,128,128]{3,2,1,0:T(8,128)(2,1)S(1)}, u32[]{:S(2)}, u32[]{:S(2)}) collective-permute-start(bf16[4,1,128,128]{3,2,1,0:T(8,128)(2,1)S(1)} %get-tuple-element.26), channel_id=1, source_target_pairs={{1,0},{3,2},{5,4},{7,6},{9,8},{11,10},{13,12},{15,14},{17,16},{19,... | collective-permute-start | bytes 393224 | tf_op jit(solution)/shard_map/ppermute | solution.py:23
  17.5 1.2 %collective-permute-done.1 = bf16[4,1,128,128]{3,2,1,0:T(8,128)(2,1)S(1)} collective-permute-done((bf16[4,1,128,128]{3,2,1,0:T(8,128)(2,1)S(1)}, bf16[4,1,128,128]{3,2,1,0:T(8,128)(2,1)S(1)}, u32[]{:S(2)}, u32[]{:S(2)}) %collective-permute-start.1) | collective-permute-done | bytes 131104 | tf_op jit(solution)/shard_map/ppermute | solution.py:21
  18.7 4.4 %collective-permute-done.2 = bf16[4,1,128,128]{3,2,1,0:T(8,128)(2,1)S(1)} collective-permute-done((bf16[4,1,128,128]{3,2,1,0:T(8,128)(2,1)S(1)}, bf16[4,1,128,128]{3,2,1,0:T(8,128)(2,1)S(1)}, u32[]{:S(2)}, u32[]{:S(2)}) %collective-permute-start.2) | collective-permute-done | bytes 131104 | tf_op jit(solution)/shard_map/ppermute | solution.py:23
  23.1 0.6 fusion.12
  23.7 0.9 %fusion.96 = (bf16[4,10,128,128]{3,2,1,0:T(8,128)(2,1)S(1)}, bf16[4,10,128,128]{3,2,1,0:T(8,128)(2,1)S(1)}) fusion(bf16[4,10,130,128]{3,2,1,0:T(8,128)(2,1)S(1)} %fusion.12), kind=kLoop, calls=%fused_computation.117 | loop fusion | bytes 5242880 | tf_op jit(solution)/shard_map/slice | solution.py:36
  24.6 0.7 pad_maximum_fusion
  25.3 2.7 %fusion.94 = (bf16[2,8,128,384]{3,2,1,0:T(8,128)(2,1)S(1)}, bf16[2,8,128,384]{3,2,1,0:T(8,128)(2,1)S(1)}, bf16[2,8,128,384]{3,2,1,0:T(8,128)(2,1)S(1)}, bf16[2,8...) fusion(bf16[4,10,128,384]{3,2,1,0:T(8,128)(2,1)S(1)} %pad_maxim, ...), kind=kLoop, calls=%fused_computation.115 | loop fusion | bytes 28311552 | tf_op jit(solution)/shard_map/slice | solution.py:45
  28.1 0.6 fusion.68
  28.7 0.6 fusion.70
  29.2 0.6 fusion.72
  29.8 0.6 fusion.74
  30.4 0.6 fusion.76
  31.0 0.6 fusion.78
  31.5 0.6 fusion.80
  32.1 0.6 fusion.82
  32.7 0.9 %fusion.22 = f32[2048,128]{1,0:T(8,128)S(1)} fusion(f32[2048,128]{1,0:T(8,128)S(1)} %fusion.68, f32[2048,128]{1,0:T(8,128)S(1)} %fusion.70, f32[2048,128]{1,0:T(8,128)S(1)} %fusion.72, f32[2048,128]{1,0:T(8,128)S(1)} %fusion.74, f32[2048,128]{1,0:T(8,128)S(1)} %fusion.76, f32[2048,128]{1,0:T(8,128)S(1)} %fusion.78, f32[2048,128]{1,0:T(8,128)S(1)} %fusion.80, ...), kind=kOutput, calls=%fused_computation.33 | convolution fusion | flops 204996608 | bytes 11108352 | tf_op jit(solution)/shard_map/dot_general | solution.py:48
  33.7 1.3 %collective-permute-start.3 = (bf16[1,128,128]{2,1,0:T(8,128)(2,1)S(1)}, bf16[1,128,128]{2,1,0:T(8,128)(2,1)S(1)}, u32[]{:S(2)}, u32[]{:S(2)}) collective-permute-start(bf16[1,128,128]{2,1,0:T(8,128)(2,1)S(1)} %slice_bitcast_fusion), channel_id=1, source_target_pairs={{1,0},{3,2},{5,4},{7,6},{9,8},{11,10},{13,12},{15,14},{17,16},{19,... | collective-permute-start | bytes 98312 | tf_op jit(solution)/shard_map/ppermute | solution.py:10
  35.0 4.5 %collective-permute-done.3 = bf16[1,128,128]{2,1,0:T(8,128)(2,1)S(1)} collective-permute-done((bf16[1,128,128]{2,1,0:T(8,128)(2,1)S(1)}, bf16[1,128,128]{2,1,0:T(8,128)(2,1)S(1)}, u32[]{:S(2)}, u32[]{:S(2)}) %collective-permute-start.3) | collective-permute-done | bytes 32800 | tf_op jit(solution)/shard_map/ppermute | solution.py:10
  39.5 0.3 slice.202
  39.9 0.3 slice.201
  40.3 0.5 slice.203
  40.9 0.2 fusion.63
  41.3 0.2 fusion.21
  41.6 1.9 %collective-permute-start.4 = (bf16[1,4,64,256]{3,2,1,0:T(8,128)(2,1)S(1)}, bf16[1,4,64,256]{3,2,1,0:T(8,128)(2,1)S(1)}, u32[]{:S(2)}, u32[]{:S(2)}) collective-permute-start(bf16[1,4,64,256]{3,2,1,0:T(8,128)(2,1)S(1)} %bitcast.122), channel_id=1, source_target_pairs={{0,2},{2,4},{4,6},{6,8},{8,10},{10,12},{12,14},{14,16},{16,18},{18... | collective-permute-start | bytes 393224 | tf_op jit(solution)/shard_map/ppermute | solution.py:10
  43.5 5.3 %collective-permute-done.4 = bf16[1,4,64,256]{3,2,1,0:T(8,128)(2,1)S(1)} collective-permute-done((bf16[1,4,64,256]{3,2,1,0:T(8,128)(2,1)S(1)}, bf16[1,4,64,256]{3,2,1,0:T(8,128)(2,1)S(1)}, u32[]{:S(2)}, u32[]{:S(2)}) %collective-permute-start.4) | collective-permute-done | bytes 131104 | tf_op jit(solution)/shard_map/ppermute | solution.py:10
  48.7 1.9 %collective-permute-start.5 = (bf16[1,4,64,256]{3,2,1,0:T(8,128)(2,1)S(1)}, bf16[1,4,64,256]{3,2,1,0:T(8,128)(2,1)S(1)}, u32[]{:S(2)}, u32[]{:S(2)}) collective-permute-start(bf16[1,4,64,256]{3,2,1,0:T(8,128)(2,1)S(1)} %collective-permute-done.4), channel_id=1, source_target_pairs={{0,2},{2,4},{4,6},{6,8},{8,10},{10,12},{12,14},{14,16},{16,18},{18... | collective-permute-start | bytes 393224 | tf_op jit(solution)/shard_map/ppermute | solution.py:10
  50.7 5.3 %collective-permute-done.5 = bf16[1,4,64,256]{3,2,1,0:T(8,128)(2,1)S(1)} collective-permute-done((bf16[1,4,64,256]{3,2,1,0:T(8,128)(2,1)S(1)}, bf16[1,4,64,256]{3,2,1,0:T(8,128)(2,1)S(1)}, u32[]{:S(2)}, u32[]{:S(2)}) %collective-permute-start.5) | collective-permute-done | bytes 131104 | tf_op jit(solution)/shard_map/ppermute | solution.py:10
  55.9 1.6 %collective-permute-start.6 = (bf16[3,1,64,256]{3,2,1,0:T(8,128)(2,1)S(1)}, bf16[3,1,64,256]{3,2,1,0:T(8,128)(2,1)S(1)}, u32[]{:S(2)}, u32[]{:S(2)}) collective-permute-start(bf16[3,1,64,256]{3,2,1,0:T(8,128)(2,1)S(1)} %get-tuple-element.32), channel_id=1, source_target_pairs={{0,1},{2,3},{4,5},{6,7},{8,9},{10,11},{12,13},{14,15},{16,17},{18,... | collective-permute-start | bytes 294920 | tf_op jit(solution)/shard_map/ppermute | solution.py:21
  57.6 1.3 %collective-permute-start.7 = (bf16[3,1,64,256]{3,2,1,0:T(8,128)(2,1)S(1)}, bf16[3,1,64,256]{3,2,1,0:T(8,128)(2,1)S(1)}, u32[]{:S(2)}, u32[]{:S(2)}) collective-permute-start(bf16[3,1,64,256]{3,2,1,0:T(8,128)(2,1)S(1)} %get-tuple-element.33), channel_id=1, source_target_pairs={{1,0},{3,2},{5,4},{7,6},{9,8},{11,10},{13,12},{15,14},{17,16},{19,... | collective-permute-start | bytes 294920 | tf_op jit(solution)/shard_map/ppermute | solution.py:23
  58.9 0.9 %collective-permute-done.6 = bf16[3,1,64,256]{3,2,1,0:T(8,128)(2,1)S(1)} collective-permute-done((bf16[3,1,64,256]{3,2,1,0:T(8,128)(2,1)S(1)}, bf16[3,1,64,256]{3,2,1,0:T(8,128)(2,1)S(1)}, u32[]{:S(2)}, u32[]{:S(2)}) %collective-permute-start.6) | collective-permute-done | bytes 98336 | tf_op jit(solution)/shard_map/ppermute | solution.py:21
  59.8 4.3 %collective-permute-done.7 = bf16[3,1,64,256]{3,2,1,0:T(8,128)(2,1)S(1)} collective-permute-done((bf16[3,1,64,256]{3,2,1,0:T(8,128)(2,1)S(1)}, bf16[3,1,64,256]{3,2,1,0:T(8,128)(2,1)S(1)}, u32[]{:S(2)}, u32[]{:S(2)}) %collective-permute-start.7) | collective-permute-done | bytes 98336 | tf_op jit(solution)/shard_map/ppermute | solution.py:23
  64.1 0.3 select_maximum_fusion
  64.4 0.3 fusion.98
  64.9 0.4 fusion.95
  65.3 1.6 %copy-done = bf16[3,3,768,256]{3,2,1,0:T(8,128)(2,1)S(1)} copy-done((bf16[3,3,768,256]{3,2,1,0:T(8,128)(2,1)S(1)}, bf16[3,3,768,256]{3,2,1,0:T(8,128)(2,1)}, u32[]{:S(2)}) %copy-start) | copy-done | bytes 3538968
  66.9 0.3 fusion.32
  67.2 0.3 fusion.34
  67.5 0.3 fusion.36
  67.8 0.3 fusion.38
  68.0 0.3 fusion.40
  68.3 0.3 fusion.42
  68.6 0.3 fusion.44
  68.9 0.3 fusion.46
  69.1 1.0 %multiply_convert_fusion.1 = bf16[256,256]{1,0:T(8,128)(2,1)} fusion(f32[256,256]{1,0:T(8,128)S(1)} %fusion.32, f32[256,256]{1,0:T(8,128)S(1)} %fusion.34, f32[256,256]{1,0:T(8,128)S(1)} %fusion.36, f32[256,256]{1,0:T(8,128)S(1)} %fusion.38, f32[256,256]{1,0:T(8,128)S(1)} %fusion.40, f32[256,256]{1,0:T(8,128)S(1)} %fusion.42, f32[256,256]{1,0:T(8,128)S(1)} %fusion.44, ...), kind=kOutput, calls=%fused_computation.75 | convolution fusion | flops 101515264 | bytes 3014656 | tf_op jit(solution)/shard_map/dot_general | solution.py:48
  (15 shorter events, 0.7 us)
Async XLA Ops:
  0.0 11.6 %collective-permute-start = (bf16[2,8,128,128]{3,2,1,0:T(8,128)(2,1)}, bf16[2,8,128,128]{3,2,1,0:T(8,128)(2,1)S(1)}, u32[]{:S(2)}, u32[]{:S(2)}) collective-permute-start(bf16[2,8,128,128]{3,2,1,0:T(8,128)(2,1)} %param.4), channel_id=1, source_target_pairs={{0,2},{2,4},{4,6},{6,8},{8,10},{10,12},{12,14},{14,16},{16,18},{18... | collective-permute-start | bytes 1572872 | tf_op jit(solution)/shard_map/ppermute | solution.py:10
  12.8 5.9 %collective-permute-start.1 = (bf16[4,1,128,128]{3,2,1,0:T(8,128)(2,1)S(1)}, bf16[4,1,128,128]{3,2,1,0:T(8,128)(2,1)S(1)}, u32[]{:S(2)}, u32[]{:S(2)}) collective-permute-start(bf16[4,1,128,128]{3,2,1,0:T(8,128)(2,1)S(1)} %get-tuple-element.25), channel_id=1, source_target_pairs={{0,1},{2,3},{4,5},{6,7},{8,9},{10,11},{12,13},{14,15},{16,17},{18,... | collective-permute-start | bytes 393224 | tf_op jit(solution)/shard_map/ppermute | solution.py:21
  16.2 6.9 %collective-permute-start.2 = (bf16[4,1,128,128]{3,2,1,0:T(8,128)(2,1)S(1)}, bf16[4,1,128,128]{3,2,1,0:T(8,128)(2,1)S(1)}, u32[]{:S(2)}, u32[]{:S(2)}) collective-permute-start(bf16[4,1,128,128]{3,2,1,0:T(8,128)(2,1)S(1)} %get-tuple-element.26), channel_id=1, source_target_pairs={{1,0},{3,2},{5,4},{7,6},{9,8},{11,10},{13,12},{15,14},{17,16},{19,... | collective-permute-start | bytes 393224 | tf_op jit(solution)/shard_map/ppermute | solution.py:23
  25.3 2.8 %copy-start.1 = (bf16[3,3,384,128]{3,2,1,0:T(8,128)(2,1)S(1)}, bf16[3,3,384,128]{3,2,1,0:T(8,128)(2,1)}, u32[]{:S(2)}) copy-start(bf16[3,3,384,128]{3,2,1,0:T(8,128)(2,1)} %param.5) | copy-start | bytes 2654212
  33.7 5.8 %collective-permute-start.3 = (bf16[1,128,128]{2,1,0:T(8,128)(2,1)S(1)}, bf16[1,128,128]{2,1,0:T(8,128)(2,1)S(1)}, u32[]{:S(2)}, u32[]{:S(2)}) collective-permute-start(bf16[1,128,128]{2,1,0:T(8,128)(2,1)S(1)} %slice_bitcast_fusion), channel_id=1, source_target_pairs={{1,0},{3,2},{5,4},{7,6},{9,8},{11,10},{13,12},{15,14},{17,16},{19,... | collective-permute-start | bytes 98312 | tf_op jit(solution)/shard_map/ppermute | solution.py:10
  39.5 1.3 %copy-start.2 = (bf16[3,384,256]{2,1,0:T(8,128)(2,1)S(1)}, bf16[3,384,256]{2,1,0:T(8,128)(2,1)}, u32[]{:S(2)}) copy-start(bf16[3,384,256]{2,1,0:T(8,128)(2,1)} %param.6) | copy-start | bytes 1769476
  41.6 7.2 %collective-permute-start.4 = (bf16[1,4,64,256]{3,2,1,0:T(8,128)(2,1)S(1)}, bf16[1,4,64,256]{3,2,1,0:T(8,128)(2,1)S(1)}, u32[]{:S(2)}, u32[]{:S(2)}) collective-permute-start(bf16[1,4,64,256]{3,2,1,0:T(8,128)(2,1)S(1)} %bitcast.122), channel_id=1, source_target_pairs={{0,2},{2,4},{4,6},{6,8},{8,10},{10,12},{12,14},{14,16},{16,18},{18... | collective-permute-start | bytes 393224 | tf_op jit(solution)/shard_map/ppermute | solution.py:10
  48.7 7.2 %collective-permute-start.5 = (bf16[1,4,64,256]{3,2,1,0:T(8,128)(2,1)S(1)}, bf16[1,4,64,256]{3,2,1,0:T(8,128)(2,1)S(1)}, u32[]{:S(2)}, u32[]{:S(2)}) collective-permute-start(bf16[1,4,64,256]{3,2,1,0:T(8,128)(2,1)S(1)} %collective-permute-done.4), channel_id=1, source_target_pairs={{0,2},{2,4},{4,6},{6,8},{8,10},{10,12},{12,14},{14,16},{16,18},{18... | collective-permute-start | bytes 393224 | tf_op jit(solution)/shard_map/ppermute | solution.py:10
  55.9 3.8 %collective-permute-start.6 = (bf16[3,1,64,256]{3,2,1,0:T(8,128)(2,1)S(1)}, bf16[3,1,64,256]{3,2,1,0:T(8,128)(2,1)S(1)}, u32[]{:S(2)}, u32[]{:S(2)}) collective-permute-start(bf16[3,1,64,256]{3,2,1,0:T(8,128)(2,1)S(1)} %get-tuple-element.32), channel_id=1, source_target_pairs={{0,1},{2,3},{4,5},{6,7},{8,9},{10,11},{12,13},{14,15},{16,17},{18,... | collective-permute-start | bytes 294920 | tf_op jit(solution)/shard_map/ppermute | solution.py:21
  57.6 6.5 %collective-permute-start.7 = (bf16[3,1,64,256]{3,2,1,0:T(8,128)(2,1)S(1)}, bf16[3,1,64,256]{3,2,1,0:T(8,128)(2,1)S(1)}, u32[]{:S(2)}, u32[]{:S(2)}) collective-permute-start(bf16[3,1,64,256]{3,2,1,0:T(8,128)(2,1)S(1)} %get-tuple-element.33), channel_id=1, source_target_pairs={{1,0},{3,2},{5,4},{7,6},{9,8},{11,10},{13,12},{15,14},{17,16},{19,... | collective-permute-start | bytes 294920 | tf_op jit(solution)/shard_map/ppermute | solution.py:23
  64.9 2.0 %copy-start = (bf16[3,3,768,256]{3,2,1,0:T(8,128)(2,1)S(1)}, bf16[3,3,768,256]{3,2,1,0:T(8,128)(2,1)}, u32[]{:S(2)}) copy-start(bf16[3,3,768,256]{3,2,1,0:T(8,128)(2,1)} %param.7) | copy-start | bytes 10616836
where the time goes:
time: 70.5 us; the launch traced here: 70.2 us
  waiting for transfers between devices  35.5 us (50%)
  starting transfers between devices  14.7 us (21%)
  matrix products  9.3 us (13%)
  local copies, waits for them, and re-layouts  8.39 us (12%)
  other arithmetic  1.92 us (3%)
    ppermute x4, waiting for transfers between devices, shifted(): lax.ppermute(value, axis, [(source, source + steps) for source in range(f...  24.7 us
    ppermute x2, waiting for transfers between devices, padded_2(): lax.ppermute(head, axis, [((i + 1) % count, i) for i in range(ends)])  8.68 us
    dot_general x18, matrix products, conv_block(): jnp.dot(window, weight[time_tap, row_tap], preferred_element_type=jnp.flo...  8.64 us
    ppermute x4, starting transfers between devices, shifted(): lax.ppermute(value, axis, [(source, source + steps) for source in range(f...  7.03 us
    ppermute x2, starting transfers between devices, padded_2(): lax.ppermute(tail, axis, [(i, (i + 1) % count) for i in range(ends)])  5.06 us
    slice x2, local copies, waits for them, and re-layouts, conv_block(): stacked[time_tap:time_tap + frames_out, row_tap:row_tap + rows_out]  3.16 us
    ppermute x2, starting transfers between devices, padded_2(): lax.ppermute(head, axis, [((i + 1) % count, i) for i in range(ends)])  2.58 us
    ppermute x2, waiting for transfers between devices, padded_2(): lax.ppermute(tail, axis, [(i, (i + 1) % count) for i in range(ends)])  2.09 us
  transfers between devices with their start and end apart: 8, of which 8 were waited for; matrix products, arithmetic and copies ran while one was open for 0% of the time, Pallas kernels for 0%

commit v1 on v0

v1 whole, which is shorter than its diff:
```python
import functools

import jax
import jax.numpy as jnp
from jax import lax
from jax.experimental import pallas as pl
from jax.experimental.pallas import tpu as pltpu
from jax.sharding import PartitionSpec as P

F32 = jnp.float32
BF16 = jnp.bfloat16


def moved(value, steps, hop):
    tm, rows = lax.axis_size("tm"), lax.axis_size("rows")
    pairs = [
        (t * rows + r, (t + steps) * rows + r + hop)
        for t in range(tm - steps)
        for r in range(rows)
        if 0 <= r + hop < rows
    ]
    return lax.ppermute(value, ("tm", "rows"), pairs)


def swapped(value, steps):
    tm = lax.axis_size("tm")
    pairs = [(t * 2 + r, (t + steps) * 2 + 1 - r) for t in range(tm - steps) for r in range(2)]
    return lax.ppermute(value, ("tm", "rows"), pairs)


def rims(cells, dim, above, below, steps):
    count = cells.shape[dim]
    if lax.axis_size("rows") == 2:
        width = max(above, below)
        first = jnp.where(lax.axis_index("rows") == 0, count - width, 0)
        both = swapped(lax.dynamic_slice_in_dim(cells, first, width, axis=dim), steps)
        return both, both
    head = lax.slice_in_dim(cells, 0, below, axis=dim)
    tail = lax.slice_in_dim(cells, count - above, count, axis=dim)
    return moved(tail, steps, 1), moved(head, steps, -1)


def shifted_columns(flat, cols):
    wide = flat.astype(F32)
    column = lax.broadcasted_iota(jnp.int32, wide.shape, 0) % cols
    left = jnp.where(column == 0, 0.0, pltpu.roll(wide, 1, 0))
    right = jnp.where(column == cols - 1, 0.0, pltpu.roll(wide, wide.shape[0] - 1, 0))
    return left.astype(BF16), right.astype(BF16)


def put_taps(taps, first, lanes, flat, cols):
    channels = flat.shape[1]
    left, right = shifted_columns(flat, cols)
    size = flat.shape[0]
    for tap, part in enumerate((left, flat, right)):
        taps[first : first + size, lanes + tap * channels : lanes + (tap + 1) * channels] = part


def fill_fine(edges, frames, above, below, taps):
    frame_count, rows, cols, channels = frames.shape
    for f in range(frame_count):
        lanes = f * 3 * channels
        top = above[f, above.shape[1] - 1]
        top = jnp.where(edges[0] != 0, top, jnp.zeros_like(top))
        put_taps(taps, 0, lanes, top, cols)
        put_taps(taps, cols, lanes, frames[f].reshape(rows * cols, channels), cols)
        low = below[f, 0:2].reshape(2 * cols, channels)
        low = jnp.where(edges[1] != 0, low, jnp.zeros_like(low))
        put_taps(taps, (rows + 1) * cols, lanes, low, cols)


def fine_sum(taps, weight, first_tap, size, cols):
    total = None
    for b in range(3):
        zero = jnp.zeros_like(weight[0, b])
        pick = lambda tap: weight[tap, b] if 0 <= tap <= 2 else zero
        right = jnp.concatenate(
            [
                jnp.concatenate([pick(first_tap), pick(first_tap - 1)], axis=1),
                jnp.concatenate([pick(first_tap + 1), pick(first_tap)], axis=1),
            ],
            axis=0,
        )
        part = jnp.dot(taps[b * cols : b * cols + size], right, preferred_element_type=F32)
        total = part if total is None else total + part
    return total


def fine_own_kernel(edges, frames, above, below, weight, out, taps):
    cols = frames.shape[2]
    fill_fine(edges, frames, above, below, taps)
    out[...] = fine_sum(taps, weight, 2, out.shape[0], cols)


def silu(v):
    return v / (1.0 + jnp.exp(-v))


def fine_rest_kernel(edges, frames, above, below, weight, own, down, out, taps, pooled):
    _, rows, cols, channels = frames.shape
    fill_fine(edges, frames, above, below, taps)
    total = own[...] + fine_sum(taps, weight, 0, own.shape[0], cols)
    fine = silu(total).astype(BF16).astype(F32)
    mean = ((fine[:, :channels] + fine[:, channels:]) * 0.5).astype(BF16).astype(F32)
    pad = pooled.shape[1] - cols
    for r in range(rows + 1):
        row = mean[r * cols : (r + 1) * cols]
        if r == rows:
            row = jnp.where(edges[1] != 0, row, 0.0)
        pooled[r, 0:cols] = row
        pooled[r, cols : cols + pad] = jnp.zeros((pad, channels), F32)
    strips = []
    for p in range(rows // 2):
        pieces = [
            pooled[2 * p + b, pl.ds(e, cols // 2, stride=2), :].astype(BF16)
            for b in range(3)
            for e in range(3)
        ]
        strips.append(jnp.concatenate(pieces, axis=1))
    left = jnp.concatenate(strips, axis=0)
    right = down[...].reshape(-1, down.shape[-1])
    out[...] = jnp.dot(left, right, preferred_element_type=F32).astype(BF16).reshape(out.shape)


def coarse_kernel(edges, *refs):
    fields, weight, out, taps = refs[:9], refs[9], refs[10], refs[11]
    half_rows, half_cols, channels = fields[0].shape[1:]
    total = None
    for a in range(3):
        body, above, below = fields[3 * a : 3 * a + 3]
        top = above[0, 0]
        top = jnp.where(edges[0] != 0, top, jnp.zeros_like(top))
        low = below[0, 0]
        low = jnp.where(edges[1] != 0, low, jnp.zeros_like(low))
        flat = body[0].reshape(half_rows * half_cols, channels)
        put_taps(taps, 0, 0, top, half_cols)
        put_taps(taps, half_cols, 0, flat, half_cols)
        put_taps(taps, (half_rows + 1) * half_cols, 0, low, half_cols)
        for b in range(3):
            left = taps[b * half_cols : (b + half_rows) * half_cols]
            part = jnp.dot(left, weight[a, b], preferred_element_type=F32)
            total = part if total is None else total + part
    out[...] = silu(total).astype(BF16).reshape(out.shape)


def call(kernel, out_shape, scratch, flops, args):
    size = sum(a.size * a.dtype.itemsize for a in args)
    specs = [pl.BlockSpec(memory_space=pltpu.SMEM)]
    specs += [pl.BlockSpec(memory_space=pltpu.VMEM)] * (len(args) - 1)
    return pl.pallas_call(
        kernel,
        out_shape=out_shape,
        in_specs=specs,
        out_specs=pl.BlockSpec(memory_space=pltpu.VMEM),
        scratch_shapes=scratch,
        cost_estimate=pl.CostEstimate(flops=flops, bytes_accessed=size, transcendentals=0),
        compiler_params=pltpu.CompilerParams(vmem_limit_bytes=40 * 1024 * 1024),
    )(*args)


def local(frames, conv_fine, conv_down, conv_coarse):
    _, rows, cols, channels = frames.shape
    wide = conv_down.shape[-1]
    strip, strips = lax.axis_index("rows"), lax.axis_size("rows")
    edges = jnp.stack([strip > 0, strip < strips - 1]).astype(jnp.int32)

    earlier = moved(frames, 1, 0)
    above, below = rims(frames, 1, 1, 2, 0)
    above_1, below_1 = rims(frames, 1, 1, 2, 1)
    size = (rows + 1) * cols
    taps = pltpu.VMEM(((rows + 3) * cols, 6 * channels), BF16)
    flops = 2 * size * 18 * channels * 2 * channels
    own = call(
        fine_own_kernel,
        jax.ShapeDtypeStruct((size, 2 * channels), F32),
        [taps],
        flops,
        (edges, frames, above, below, conv_fine),
    )
    half_rows, half_cols = rows // 2, cols // 2
    reduced = call(
        fine_rest_kernel,
        jax.ShapeDtypeStruct((1, half_rows, half_cols, wide), BF16),
        [taps, pltpu.VMEM((rows + 1, cols + 8, channels), F32)],
        flops,
        (edges, earlier, above_1, below_1, conv_fine, own, conv_down),
    )
    back_2 = moved(reduced, 2, 0)
    back_1 = moved(reduced, 1, 0)
    fields = []
    for steps, body in ((2, back_2), (1, back_1), (0, reduced)):
        fields += [body, *rims(reduced, 1, 1, 1, steps)]
    return call(
        coarse_kernel,
        jax.ShapeDtypeStruct((1, half_rows, half_cols, wide), BF16),
        [pltpu.VMEM(((half_rows + 2) * half_cols, 3 * wide), BF16)],
        2 * half_rows * half_cols * 27 * wide * wide,
        (edges, *fields, conv_coarse),
    )


def solution(mesh):
    placed = (P("tm", "rows", None, None), P(), P(), P())
    return jax.shard_map(
        local, mesh=mesh, in_specs=placed, out_specs=P("tm", "rows", None, None), check_vma=False
    )
```

time: 70.5 us -> 37.3 us (0.53)
  waiting for transfers between devices: 35.5 us -> 6.63 us
  matrix products: 9.3 us -> 0 us
  Pallas kernels: 0 us -> 7.47 us
  local copies, waits for them, and re-layouts: 8.39 us -> 3.16 us
  starting transfers between devices: 14.7 us -> 19.5 us
  other arithmetic: 1.92 us -> 0.08 us
    ppermute x8, waiting for transfers between devices: 35.5 us -> 6.63 us  [the longest x5 6.62 us: swapped(): return lax.ppermute(value, ('tm', 'rows'), pairs)]
    dot_general x21 -> x0, matrix products: 9.3 us -> none  [the longest x18 8.64 us: conv_block(): jnp.dot(window, weight[time_tap, row_tap], preferred_element_type=jnp.flo...]
    pallas_call x0 -> x3, Pallas kernels: none -> 7.47 us  [call(): pl.pallas_call(kernel, out_shape=out_shape, in_specs=specs, out_specs=pl....]
    slice x10 -> x0, local copies, waits for them, and re-layouts: 5.64 us -> none  [the longest x2 3.16 us: conv_block(): stacked[time_tap:time_tap + frames_out, row_tap:row_tap + rows_out]]
    ppermute x8, starting transfers between devices: 14.7 us -> 19.5 us  [the longest x5 12.5 us: swapped(): return lax.ppermute(value, ('tm', 'rows'), pairs)]
    concatenate x6 -> x0, other arithmetic: 1.84 us -> none  [the longest x2 0.88 us: padded_2(): jnp.concatenate([lax.ppermute(tail, axis, [(i, (i + 1) % count) for i in...]
    concatenate x1 -> x0, local copies, waits for them, and re-layouts: 1.12 us -> none  [local(): joined = jnp.concatenate([earlier, frames], axis=0)]
    dynamic_slice x0 -> x2, local copies, waits for them, and re-layouts: none -> 0.94 us  [rims(): lax.dynamic_slice_in_dim(cells, first, width, axis=dim)]
  transfers between devices with their start and end apart: 8 -> 8, of which waited for: 8 -> 4; matrix products, arithmetic and copies ran while one was open for 0% -> 3% of each run, Pallas kernels for 0% -> 6%
where the time goes in v1:
time: 37.3 us; the launch traced here: 37 us
  starting transfers between devices  19.5 us (52%)
  Pallas kernels  7.47 us (20%)
  waiting for transfers between devices  6.63 us (18%)
  local copies, waits for them, and re-layouts  3.16 us (8%)
    ppermute x5, starting transfers between devices, swapped(): return lax.ppermute(value, ('tm', 'rows'), pairs)  12.5 us
    pallas_call x3, Pallas kernels, call(): pl.pallas_call(kernel, out_shape=out_shape, in_specs=specs, out_specs=pl....  7.47 us
    ppermute x3, starting transfers between devices, moved(): return lax.ppermute(value, ('tm', 'rows'), pairs)  7.06 us
    ppermute x5, waiting for transfers between devices, swapped(): return lax.ppermute(value, ('tm', 'rows'), pairs)  6.62 us
    unnamed x10, local copies, waits for them, and re-layouts  2.22 us
    dynamic_slice x2, local copies, waits for them, and re-layouts, rims(): lax.dynamic_slice_in_dim(cells, first, width, axis=dim)  0.94 us
  transfers between devices with their start and end apart: 8, of which 4 were waited for; matrix products, arithmetic and copies ran while one was open for 3% of the time, Pallas kernels for 6%

profile of v1, /device:TPU:16, one launch (start us, length us, event | category | flops | bytes accessed | tf_op | source)
XLA Modules:
  0.0 37.0 jit_solution(6411992851278496380)
XLA Ops:
  0.0 1.9 %collective-permute-start = (bf16[2,8,128,128]{3,2,1,0:T(8,128)(2,1)}, bf16[2,8,128,128]{3,2,1,0:T(8,128)(2,1)S(1)}, u32[]{:S(2)}, u32[]{:S(2)}) collective-permute-start(bf16[2,8,128,128]{3,2,1,0:T(8,128)(2,1)} %frames.1), channel_id=1, source_target_pairs={{0,2},{1,3},{2,4},{3,5},{4,6},{5,7},{6,8},{7,9},{8,10},{9,11},{10,... | collective-permute-start | bytes 1572872 | tf_op jit(solution)/shard_map/ppermute | solution.py:22
  1.9 0.9 %constant_dynamic-slice_fusion.1 = bf16[2,2,128,128]{3,2,1,0:T(8,128)(2,1)S(1)} fusion(bf16[2,8,128,128]{3,2,1,0:T(8,128)(2,1)} %frames.1, s32[]{:T(128)S(6)} %select_n.15), kind=kLoop, calls=%fused_computation.2 | loop fusion | bytes 262148 | tf_op jit(solution)/shard_map/dynamic_slice | solution.py:36
  2.9 1.6 %collective-permute-start.2 = (bf16[2,2,128,128]{3,2,1,0:T(8,128)(2,1)S(1)}, bf16[2,2,128,128]{3,2,1,0:T(8,128)(2,1)S(1)}, u32[]{:S(2)}, u32[]{:S(2)}) collective-permute-start(bf16[2,2,128,128]{3,2,1,0:T(8,128)(2,1)S(1)} %constant_dynamic-slice_fusion.1), channel_id=1, source_target_pairs={{0,1},{1,0},{2,3},{3,2},{4,5},{5,4},{6,7},{7,6},{8,9},{9,8},{10,11... | collective-permute-start | bytes 393224 | tf_op jit(solution)/shard_map/ppermute | solution.py:28
  4.4 3.4 %collective-permute-start.1 = (bf16[2,2,128,128]{3,2,1,0:T(8,128)(2,1)S(1)}, bf16[2,2,128,128]{3,2,1,0:T(8,128)(2,1)S(1)}, u32[]{:S(2)}, u32[]{:S(2)}) collective-permute-start(bf16[2,2,128,128]{3,2,1,0:T(8,128)(2,1)S(1)} %constant_dynamic-slice_fusion.1), channel_id=1, source_target_pairs={{0,3},{1,2},{2,5},{3,4},{4,7},{5,6},{6,9},{7,8},{8,11},{9,10},{10,... | collective-permute-start | bytes 393224 | tf_op jit(solution)/shard_map/ppermute | solution.py:28
  7.8 0.1 add_convert_fusion.edges
  7.9 0.8 %collective-permute-done.2.above.below = bf16[2,2,128,128]{3,2,1,0:T(8,128)(2,1)S(1)} collective-permute-done((bf16[2,2,128,128]{3,2,1,0:T(8,128)(2,1)S(1)}, bf16[2,2,128,128]{3,2,1,0:T(8,128)(2,1)S(1)}, u32[]{:S(2)}, u32[]{:S(2)}) %collective-permute-start.2) | collective-permute-done | bytes 131104 | tf_op jit(solution)/shard_map/ppermute | solution.py:28
  8.6 0.0 copy-start.1
  8.6 1.0 %copy-done.1 = bf16[2,8,128,128]{3,2,1,0:T(8,128)(2,1)S(1)} copy-done((bf16[2,8,128,128]{3,2,1,0:T(8,128)(2,1)S(1)}, bf16[2,8,128,128]{3,2,1,0:T(8,128)(2,1)}, u32[]{:S(2)}) %copy-start.1) | copy-done | bytes 524312
  9.7 0.0 copy-start.2
  9.7 1.2 %copy-done.2 = bf16[3,3,384,128]{3,2,1,0:T(8,128)(2,1)S(1)} copy-done((bf16[3,3,384,128]{3,2,1,0:T(8,128)(2,1)S(1)}, bf16[3,3,384,128]{3,2,1,0:T(8,128)(2,1)}, u32[]{:S(2)}) %copy-start.2) | copy-done | bytes 884760
  10.8 0.0 copy-start.3
  10.8 0.0 copy-start.4
  10.8 2.1 %shard_map.46.own = f32[1152,256]{1,0:T(8,128)S(1)} custom-call(s32[2]{0:T(128)S(1)} %add_convert_fusion.edges, bf16[2,8,128,128]{3,2,1,0:T(8,128)(2,1)S(1)} %copy-done.1, bf16[2,2,128,128]{3,2,1,0:T(8,128)(2,1)S(1)} %collective-permute-done.2.above.below, bf16[2,2,128,128]{3,2,1,0:T(8,128)(2,1)S(1)} %collective-permute-done.2.above.below, ...), custom_call_target="tpu_custom_call" | custom-call | flops 1358954496 | bytes 1671176 | tf_op jit(solution)/shard_map/pallas_call | solution.py:150
  13.0 0.0 copy-start
  13.0 1.0 %collective-permute-done.1.above.below = bf16[2,2,128,128]{3,2,1,0:T(8,128)(2,1)S(1)} collective-permute-done((bf16[2,2,128,128]{3,2,1,0:T(8,128)(2,1)S(1)}, bf16[2,2,128,128]{3,2,1,0:T(8,128)(2,1)S(1)}, u32[]{:S(2)}, u32[]{:S(2)}) %collective-permute-start.1) | collective-permute-done | bytes 131104 | tf_op jit(solution)/shard_map/ppermute | solution.py:28
  14.0 0.0 collective-permute-done.frames
  14.0 0.0 copy-done.3
  14.0 0.0 copy-done.4
  14.0 3.0 %shard_map.47.refs_6_ = bf16[1,4,64,256]{3,2,1,0:T(8,128)(2,1)S(1)} custom-call(s32[2]{0:T(128)S(1)} %add_convert_fusion.edges, bf16[2,8,128,128]{3,2,1,0:T(8,128)(2,1)S(1)} %collective-permute-done.frames, bf16[2,2,128,128]{3,2,1,0:T(8,128)(2,1)S(1)} %collective-permute-done.1.above.below, bf16[2,2,128,128]{3,2,1,0:T(8,128)(2,1)S(1)} %collective-permute-done.1.above.below, ...), custom_call_target="tpu_custom_call" | custom-call | flops 1358954496 | bytes 3440648 | tf_op jit(solution)/shard_map/pallas_call | solution.py:150
  17.0 1.9 %collective-permute-start.5 = (bf16[1,4,64,256]{3,2,1,0:T(8,128)(2,1)S(1)}, bf16[1,4,64,256]{3,2,1,0:T(8,128)(2,1)S(1)}, u32[]{:S(2)}, u32[]{:S(2)}) collective-permute-start(bf16[1,4,64,256]{3,2,1,0:T(8,128)(2,1)S(1)} %shard_map.47.refs_6_), channel_id=1, source_target_pairs={{0,2},{1,3},{2,4},{3,5},{4,6},{5,7},{6,8},{7,9},{8,10},{9,11},{10,... | collective-permute-start | bytes 393224 | tf_op jit(solution)/shard_map/ppermute | solution.py:22
  18.9 3.2 %collective-permute-start.3 = (bf16[1,4,64,256]{3,2,1,0:T(8,128)(2,1)S(1)}, bf16[1,4,64,256]{3,2,1,0:T(8,128)(2,1)S(1)}, u32[]{:S(2)}, u32[]{:S(2)}) collective-permute-start(bf16[1,4,64,256]{3,2,1,0:T(8,128)(2,1)S(1)} %shard_map.47.refs_6_), channel_id=1, source_target_pairs={{0,4},{1,5},{2,6},{3,7},{4,8},{5,9},{6,10},{7,11},{8,12},{9,13},{1... | collective-permute-start | bytes 393224 | tf_op jit(solution)/shard_map/ppermute | solution.py:22
  22.2 1.6 %collective-permute-start.7 = (bf16[1,1,64,256]{3,2,1,0:T(8,128)(2,1)S(1)}, bf16[1,1,64,256]{3,2,1,0:T(8,128)(2,1)S(1)}, u32[]{:S(2)}, u32[]{:S(2)}) collective-permute-start(bf16[1,1,64,256]{3,2,1,0:T(8,128)(2,1)S(1)} %constant_dynamic-slice_fusion), channel_id=1, source_target_pairs={{0,1},{1,0},{2,3},{3,2},{4,5},{5,4},{6,7},{7,6},{8,9},{9,8},{10,11... | collective-permute-start | bytes 98312 | tf_op jit(solution)/shard_map/ppermute | solution.py:28
  23.8 3.3 %collective-permute-start.6 = (bf16[1,1,64,256]{3,2,1,0:T(8,128)(2,1)S(1)}, bf16[1,1,64,256]{3,2,1,0:T(8,128)(2,1)S(1)}, u32[]{:S(2)}, u32[]{:S(2)}) collective-permute-start(bf16[1,1,64,256]{3,2,1,0:T(8,128)(2,1)S(1)} %constant_dynamic-slice_fusion), channel_id=1, source_target_pairs={{0,3},{1,2},{2,5},{3,4},{4,7},{5,6},{6,9},{7,8},{8,11},{9,10},{10,... | collective-permute-start | bytes 98312 | tf_op jit(solution)/shard_map/ppermute | solution.py:28
  27.0 2.7 %collective-permute-start.4 = (bf16[1,1,64,256]{3,2,1,0:T(8,128)(2,1)S(1)}, bf16[1,1,64,256]{3,2,1,0:T(8,128)(2,1)S(1)}, u32[]{:S(2)}, u32[]{:S(2)}) collective-permute-start(bf16[1,1,64,256]{3,2,1,0:T(8,128)(2,1)S(1)} %constant_dynamic-slice_fusion), channel_id=1, source_target_pairs={{0,5},{1,4},{2,7},{3,6},{4,9},{5,8},{6,11},{7,10},{8,13},{9,12},{1... | collective-permute-start | bytes 98312 | tf_op jit(solution)/shard_map/ppermute | solution.py:28
  29.7 0.0 collective-permute-done.7.refs_7_.refs_8_
  29.7 1.0 %collective-permute-done.6.refs_4_.refs_5_ = bf16[1,1,64,256]{3,2,1,0:T(8,128)(2,1)S(1)} collective-permute-done((bf16[1,1,64,256]{3,2,1,0:T(8,128)(2,1)S(1)}, bf16[1,1,64,256]{3,2,1,0:T(8,128)(2,1)S(1)}, u32[]{:S(2)}, u32[]{:S(2)}) %collective-permute-start.6) | collective-permute-done | bytes 32800 | tf_op jit(solution)/shard_map/ppermute | solution.py:28
  30.8 3.9 %collective-permute-done.4.refs_1_.refs_2_ = bf16[1,1,64,256]{3,2,1,0:T(8,128)(2,1)S(1)} collective-permute-done((bf16[1,1,64,256]{3,2,1,0:T(8,128)(2,1)S(1)}, bf16[1,1,64,256]{3,2,1,0:T(8,128)(2,1)S(1)}, u32[]{:S(2)}, u32[]{:S(2)}) %collective-permute-start.4) | collective-permute-done | bytes 32800 | tf_op jit(solution)/shard_map/ppermute | solution.py:28
  34.6 0.0 collective-permute-done.5.refs_3_
  34.7 0.0 collective-permute-done.3.refs_0_
  34.7 0.0 copy-done
  34.7 2.3 %shard_map.48 = bf16[1,4,64,256]{3,2,1,0:T(8,128)(2,1)} custom-call(s32[2]{0:T(128)S(1)} %add_convert_fusion.edges, bf16[1,4,64,256]{3,2,1,0:T(8,128)(2,1)S(1)} %collective-permute-done.3.refs_0_, bf16[1,1,64,256]{3,2,1,0:T(8,128)(2,1)S(1)} %collective-permute-done.4.refs_1_.refs_2_, bf16[1,1,64,256]{3,2,1,0:T(8,128)(2,1)S(1)} %collective-permute-done.4.refs_1_.refs_2_, ...), custom_call_target="tpu_custom_call" | custom-call | flops 905969664 | bytes 4128776 | tf_op jit(solution)/shard_map/pallas_call | solution.py:150
  (1 shorter events, 0.0 us)
Async XLA Ops:
  0.0 14.0 %collective-permute-start = (bf16[2,8,128,128]{3,2,1,0:T(8,128)(2,1)}, bf16[2,8,128,128]{3,2,1,0:T(8,128)(2,1)S(1)}, u32[]{:S(2)}, u32[]{:S(2)}) collective-permute-start(bf16[2,8,128,128]{3,2,1,0:T(8,128)(2,1)} %frames.1), channel_id=1, source_target_pairs={{0,2},{1,3},{2,4},{3,5},{4,6},{5,7},{6,8},{7,9},{8,10},{9,11},{10,... | collective-permute-start | bytes 1572872 | tf_op jit(solution)/shard_map/ppermute | solution.py:22
  2.9 5.8 %collective-permute-start.2 = (bf16[2,2,128,128]{3,2,1,0:T(8,128)(2,1)S(1)}, bf16[2,2,128,128]{3,2,1,0:T(8,128)(2,1)S(1)}, u32[]{:S(2)}, u32[]{:S(2)}) collective-permute-start(bf16[2,2,128,128]{3,2,1,0:T(8,128)(2,1)S(1)} %constant_dynamic-slice_fusion.1), channel_id=1, source_target_pairs={{0,1},{1,0},{2,3},{3,2},{4,5},{5,4},{6,7},{7,6},{8,9},{9,8},{10,11... | collective-permute-start | bytes 393224 | tf_op jit(solution)/shard_map/ppermute | solution.py:28
  4.4 9.5 %collective-permute-start.1 = (bf16[2,2,128,128]{3,2,1,0:T(8,128)(2,1)S(1)}, bf16[2,2,128,128]{3,2,1,0:T(8,128)(2,1)S(1)}, u32[]{:S(2)}, u32[]{:S(2)}) collective-permute-start(bf16[2,2,128,128]{3,2,1,0:T(8,128)(2,1)S(1)} %constant_dynamic-slice_fusion.1), channel_id=1, source_target_pairs={{0,3},{1,2},{2,5},{3,4},{4,7},{5,6},{6,9},{7,8},{8,11},{9,10},{10,... | collective-permute-start | bytes 393224 | tf_op jit(solution)/shard_map/ppermute | solution.py:28
  8.6 1.0 %copy-start.1 = (bf16[2,8,128,128]{3,2,1,0:T(8,128)(2,1)S(1)}, bf16[2,8,128,128]{3,2,1,0:T(8,128)(2,1)}, u32[]{:S(2)}) copy-start(bf16[2,8,128,128]{3,2,1,0:T(8,128)(2,1)} %frames.1) | copy-start | bytes 1572868
  9.7 1.2 %copy-start.2 = (bf16[3,3,384,128]{3,2,1,0:T(8,128)(2,1)S(1)}, bf16[3,3,384,128]{3,2,1,0:T(8,128)(2,1)}, u32[]{:S(2)}) copy-start(bf16[3,3,384,128]{3,2,1,0:T(8,128)(2,1)} %weight.3) | copy-start | bytes 2654212
  10.8 3.1 %copy-start.3 = (bf16[3,3,384,128]{3,2,1,0:T(8,128)(2,1)S(1)}, bf16[3,3,384,128]{3,2,1,0:T(8,128)(2,1)}, u32[]{:S(2)}) copy-start(bf16[3,3,384,128]{3,2,1,0:T(8,128)(2,1)} %weight.3) | copy-start | bytes 2654212
  10.8 3.1 %copy-start.4 = (bf16[3,384,256]{2,1,0:T(8,128)(2,1)S(1)}, bf16[3,384,256]{2,1,0:T(8,128)(2,1)}, u32[]{:S(2)}) copy-start(bf16[3,384,256]{2,1,0:T(8,128)(2,1)} %down.1) | copy-start | bytes 1769476
  13.0 21.7 %copy-start = (bf16[3,3,768,256]{3,2,1,0:T(8,128)(2,1)S(1)}, bf16[3,3,768,256]{3,2,1,0:T(8,128)(2,1)}, u32[]{:S(2)}) copy-start(bf16[3,3,768,256]{3,2,1,0:T(8,128)(2,1)} %refs_9_.1) | copy-start | bytes 10616836
  17.0 17.7 %collective-permute-start.5 = (bf16[1,4,64,256]{3,2,1,0:T(8,128)(2,1)S(1)}, bf16[1,4,64,256]{3,2,1,0:T(8,128)(2,1)S(1)}, u32[]{:S(2)}, u32[]{:S(2)}) collective-permute-start(bf16[1,4,64,256]{3,2,1,0:T(8,128)(2,1)S(1)} %shard_map.47.refs_6_), channel_id=1, source_target_pairs={{0,2},{1,3},{2,4},{3,5},{4,6},{5,7},{6,8},{7,9},{8,10},{9,11},{10,... | collective-permute-start | bytes 393224 | tf_op jit(solution)/shard_map/ppermute | solution.py:22
  18.9 15.7 %collective-permute-start.3 = (bf16[1,4,64,256]{3,2,1,0:T(8,128)(2,1)S(1)}, bf16[1,4,64,256]{3,2,1,0:T(8,128)(2,1)S(1)}, u32[]{:S(2)}, u32[]{:S(2)}) collective-permute-start(bf16[1,4,64,256]{3,2,1,0:T(8,128)(2,1)S(1)} %shard_map.47.refs_6_), channel_id=1, source_target_pairs={{0,4},{1,5},{2,6},{3,7},{4,8},{5,9},{6,10},{7,11},{8,12},{9,13},{1... | collective-permute-start | bytes 393224 | tf_op jit(solution)/shard_map/ppermute | solution.py:22
  22.2 7.6 %collective-permute-start.7 = (bf16[1,1,64,256]{3,2,1,0:T(8,128)(2,1)S(1)}, bf16[1,1,64,256]{3,2,1,0:T(8,128)(2,1)S(1)}, u32[]{:S(2)}, u32[]{:S(2)}) collective-permute-start(bf16[1,1,64,256]{3,2,1,0:T(8,128)(2,1)S(1)} %constant_dynamic-slice_fusion), channel_id=1, source_target_pairs={{0,1},{1,0},{2,3},{3,2},{4,5},{5,4},{6,7},{7,6},{8,9},{9,8},{10,11... | collective-permute-start | bytes 98312 | tf_op jit(solution)/shard_map/ppermute | solution.py:28
  23.8 7.0 %collective-permute-start.6 = (bf16[1,1,64,256]{3,2,1,0:T(8,128)(2,1)S(1)}, bf16[1,1,64,256]{3,2,1,0:T(8,128)(2,1)S(1)}, u32[]{:S(2)}, u32[]{:S(2)}) collective-permute-start(bf16[1,1,64,256]{3,2,1,0:T(8,128)(2,1)S(1)} %constant_dynamic-slice_fusion), channel_id=1, source_target_pairs={{0,3},{1,2},{2,5},{3,4},{4,7},{5,6},{6,9},{7,8},{8,11},{9,10},{10,... | collective-permute-start | bytes 98312 | tf_op jit(solution)/shard_map/ppermute | solution.py:28
  27.0 7.6 %collective-permute-start.4 = (bf16[1,1,64,256]{3,2,1,0:T(8,128)(2,1)S(1)}, bf16[1,1,64,256]{3,2,1,0:T(8,128)(2,1)S(1)}, u32[]{:S(2)}, u32[]{:S(2)}) collective-permute-start(bf16[1,1,64,256]{3,2,1,0:T(8,128)(2,1)S(1)} %constant_dynamic-slice_fusion), channel_id=1, source_target_pairs={{0,5},{1,4},{2,7},{3,6},{4,9},{5,8},{6,11},{7,10},{8,13},{9,12},{1... | collective-permute-start | bytes 98312 | tf_op jit(solution)/shard_map/ppermute | solution.py:28

commit v2 on v1

--- a/solution.py
+++ b/solution.py
@@ -28,16 +28,32 @@
     return lax.ppermute(value, ("tm", "rows"), pairs)
 
 
-def rims(cells, dim, above, below, steps):
-    count = cells.shape[dim]
+def edge_kernel(cells, out, sem):
+    width = out.shape[1]
+    first = (1 - lax.axis_index("rows")) * (cells.shape[1] - width)
+    copy = pltpu.make_async_copy(cells.at[:, pl.ds(first, width)], out, sem)
+    copy.start()
+    copy.wait()
+
+
+def edge_rows(cells, width):
+    return pl.pallas_call(
+        edge_kernel,
+        out_shape=jax.ShapeDtypeStruct((cells.shape[0], width, *cells.shape[2:]), cells.dtype),
+        in_specs=[pl.BlockSpec(memory_space=pltpu.HBM)],
+        out_specs=pl.BlockSpec(memory_space=pltpu.VMEM),
+        scratch_shapes=[pltpu.SemaphoreType.DMA],
+        cost_estimate=pl.CostEstimate(flops=4 * 10**9, bytes_accessed=1 << 20, transcendentals=0),
+    )(cells)
+
+
+def frame_rims(frames):
+    rows = frames.shape[1]
     if lax.axis_size("rows") == 2:
-        width = max(above, below)
-        first = jnp.where(lax.axis_index("rows") == 0, count - width, 0)
-        both = swapped(lax.dynamic_slice_in_dim(cells, first, width, axis=dim), steps)
-        return both, both
-    head = lax.slice_in_dim(cells, 0, below, axis=dim)
-    tail = lax.slice_in_dim(cells, count - above, count, axis=dim)
-    return moved(tail, steps, 1), moved(head, steps, -1)
+        sent = edge_rows(frames, 2)
+        return [(both, both) for both in (swapped(sent, 0), swapped(sent, 1))]
+    head, tail = frames[:, :2], frames[:, rows - 1 :]
+    return [(moved(tail, steps, 1), moved(head, steps, -1)) for steps in (0, 1)]
 
 
 def shifted_columns(flat, cols):
@@ -87,9 +103,8 @@
 
 
 def fine_own_kernel(edges, frames, above, below, weight, out, taps):
-    cols = frames.shape[2]
     fill_fine(edges, frames, above, below, taps)
-    out[...] = fine_sum(taps, weight, 2, out.shape[0], cols)
+    out[...] = fine_sum(taps, weight, 2, out.shape[0], frames.shape[2])
 
 
 def silu(v):
@@ -122,25 +137,66 @@
     out[...] = jnp.dot(left, right, preferred_element_type=F32).astype(BF16).reshape(out.shape)
 
 
-def coarse_kernel(edges, *refs):
-    fields, weight, out, taps = refs[:9], refs[9], refs[10], refs[11]
-    half_rows, half_cols, channels = fields[0].shape[1:]
-    total = None
-    for a in range(3):
-        body, above, below = fields[3 * a : 3 * a + 3]
-        top = above[0, 0]
-        top = jnp.where(edges[0] != 0, top, jnp.zeros_like(top))
-        low = below[0, 0]
-        low = jnp.where(edges[1] != 0, low, jnp.zeros_like(low))
-        flat = body[0].reshape(half_rows * half_cols, channels)
-        put_taps(taps, 0, 0, top, half_cols)
-        put_taps(taps, half_cols, 0, flat, half_cols)
-        put_taps(taps, (half_rows + 1) * half_cols, 0, low, half_cols)
-        for b in range(3):
-            left = taps[b * half_cols : (b + half_rows) * half_cols]
-            part = jnp.dot(left, weight[a, b], preferred_element_type=F32)
-            total = part if total is None else total + part
-    out[...] = silu(total).astype(BF16).reshape(out.shape)
+def field_taps(field):
+    _, rows, cols, channels = field.shape
+    flat = field[0].reshape(rows * cols, channels)
+    left, right = shifted_columns(flat, cols)
+    return jnp.concatenate([left, flat, right], axis=1)
+
+
+def rim_sum(edges, taps, weight, a, cols, both):
+    size = taps.shape[0]
+    dot = functools.partial(jnp.dot, preferred_element_type=F32)
+    if both:
+        return [dot(taps[:cols], weight[a, 2]), dot(taps[size - cols :], weight[a, 0])]
+    row = jnp.where(edges[0] != 0, taps[:cols], taps[size - cols :])
+    return [dot(row, weight[a, 2 * edges[0]])]
+
+
+def body_sum(taps, weight, a, cols):
+    size = taps.shape[0]
+    dot = functools.partial(jnp.dot, preferred_element_type=F32)
+    zero = jnp.zeros((cols, weight.shape[-1]), F32)
+    upper = jnp.concatenate([zero, dot(taps[: size - cols], weight[a, 0])], axis=0)
+    lower = jnp.concatenate([dot(taps[cols:], weight[a, 2]), zero], axis=0)
+    return dot(taps, weight[a, 1]) + upper + lower
+
+
+def coarse_own_kernel(edges, field, weight, body, rim):
+    cols = field.shape[2]
+    taps = field_taps(field)
+    body[...] = body_sum(taps, weight, 2, cols)
+    for i, part in enumerate(rim_sum(edges, taps, weight, 2, cols, rim.shape[0] == 2)):
+        rim[i] = part
+
+
+def coarse_rim_kernel(edges, field_0, field_1, weight, own, out):
+    cols = field_0.shape[2]
+    sums = [own[i] for i in range(own.shape[0])]
+    for a, field in enumerate((field_0, field_1)):
+        parts = rim_sum(edges, field_taps(field), weight, a, cols, own.shape[0] == 2)
+        sums = [x + y for x, y in zip(sums, parts)]
+    for i, x in enumerate(sums):
+        out[i] = x.astype(BF16)
+
+
+def coarse_body_kernel(edges, field_0, field_1, weight, own, out):
+    cols = field_0.shape[2]
+    total = own[...]
+    for a, field in enumerate((field_0, field_1)):
+        total = total + body_sum(field_taps(field), weight, a, cols)
+    out[...] = total
+
+
+def finish_kernel(edges, total, above, below, out):
+    _, rows, cols, channels = out.shape
+    for p in range(rows):
+        row = total[p * cols : (p + 1) * cols]
+        if p == 0:
+            row = row + jnp.where(edges[0] != 0, above[0].astype(F32), 0.0)
+        if p == rows - 1:
+            row = row + jnp.where(edges[1] != 0, below[0].astype(F32), 0.0)
+        out[0, p] = silu(row).astype(BF16)
 
 
 def call(kernel, out_shape, scratch, flops, args):
@@ -151,7 +207,7 @@
         kernel,
         out_shape=out_shape,
         in_specs=specs,
-        out_specs=pl.BlockSpec(memory_space=pltpu.VMEM),
+        out_specs=jax.tree.map(lambda _: pl.BlockSpec(memory_space=pltpu.VMEM), out_shape),
         scratch_shapes=scratch,
         cost_estimate=pl.CostEstimate(flops=flops, bytes_accessed=size, transcendentals=0),
         compiler_params=pltpu.CompilerParams(vmem_limit_bytes=40 * 1024 * 1024),
@@ -165,8 +221,7 @@
     edges = jnp.stack([strip > 0, strip < strips - 1]).astype(jnp.int32)
 
     earlier = moved(frames, 1, 0)
-    above, below = rims(frames, 1, 1, 2, 0)
-    above_1, below_1 = rims(frames, 1, 1, 2, 1)
+    (above, below), (above_1, below_1) = frame_rims(frames)
     size = (rows + 1) * cols
     taps = pltpu.VMEM(((rows + 3) * cols, 6 * channels), BF16)
     flops = 2 * size * 18 * channels * 2 * channels
@@ -178,25 +233,41 @@
         (edges, frames, above, below, conv_fine),
     )
     half_rows, half_cols = rows // 2, cols // 2
+    field = jax.ShapeDtypeStruct((1, half_rows, half_cols, wide), BF16)
     reduced = call(
         fine_rest_kernel,
-        jax.ShapeDtypeStruct((1, half_rows, half_cols, wide), BF16),
+        field,
         [taps, pltpu.VMEM((rows + 1, cols + 8, channels), F32)],
         flops,
         (edges, earlier, above_1, below_1, conv_fine, own, conv_down),
     )
     back_2 = moved(reduced, 2, 0)
     back_1 = moved(reduced, 1, 0)
-    fields = []
-    for steps, body in ((2, back_2), (1, back_1), (0, reduced)):
-        fields += [body, *rims(reduced, 1, 1, 1, steps)]
-    return call(
-        coarse_kernel,
-        jax.ShapeDtypeStruct((1, half_rows, half_cols, wide), BF16),
-        [pltpu.VMEM(((half_rows + 2) * half_cols, 3 * wide), BF16)],
-        2 * half_rows * half_cols * 27 * wide * wide,
-        (edges, *fields, conv_coarse),
-    )
+    sums = jax.ShapeDtypeStruct((half_rows * half_cols, wide), F32)
+    sides = 1 if strips == 2 else 2
+    flops = 2 * half_rows * half_cols * 9 * wide * wide
+    own_sum, own_rim = call(
+        coarse_own_kernel,
+        (sums, jax.ShapeDtypeStruct((sides, half_cols, wide), F32)),
+        [],
+        flops,
+        (edges, reduced, conv_coarse),
+    )
+    rim = call(
+        coarse_rim_kernel,
+        jax.ShapeDtypeStruct((sides, half_cols, wide), BF16),
+        [],
+        flops // 4,
+        (edges, back_2, back_1, conv_coarse, own_rim),
+    )
+    if sides == 1:
+        from_above = from_below = swapped(rim, 0)
+    else:
+        from_above, from_below = moved(rim[1:], 0, 1), moved(rim[:1], 0, -1)
+    total = call(
+        coarse_body_kernel, sums, [], 2 * flops, (edges, back_2, back_1, conv_coarse, own_sum)
+    )
+    return call(finish_kernel, field, [], sums.size, (edges, total, from_above, from_below))
 
 
 def solution(mesh):

time: 37.3 us -> 34.3 us (0.920)
  starting transfers between devices: 19.5 us -> 13.5 us
  Pallas kernels: 7.47 us -> 11 us
  local copies, waits for them, and re-layouts: 3.16 us -> 0.02 us
  waiting for transfers between devices: 6.63 us -> 9.33 us
    ppermute x5 -> x3, starting transfers between devices: 12.5 us -> 5.93 us  [swapped(): return lax.ppermute(value, ('tm', 'rows'), pairs)]
    ppermute x3, waiting for transfers between devices: 0.01 us -> 4.22 us  [moved(): return lax.ppermute(value, ('tm', 'rows'), pairs)]
    pallas_call x3 -> x7, Pallas kernels: 7.47 us -> 11 us  [the longest x6 9.47 us: call(): pl.pallas_call(kernel, out_shape=out_shape, in_specs=specs, out_specs=jax...]
    unnamed x10 -> x8, local copies, waits for them, and re-layouts: 2.22 us -> 0.02 us
    ppermute x5 -> x3, waiting for transfers between devices: 6.62 us -> 5.11 us  [swapped(): return lax.ppermute(value, ('tm', 'rows'), pairs)]
    dynamic_slice x2 -> x0, local copies, waits for them, and re-layouts: 0.94 us -> none  [rims(): lax.dynamic_slice_in_dim(cells, first, width, axis=dim)]
    ppermute x3, starting transfers between devices: 7.06 us -> 7.57 us  [moved(): return lax.ppermute(value, ('tm', 'rows'), pairs)]
  transfers between devices with their start and end apart: 8 -> 6, of which waited for: 4 -> 5; matrix products, arithmetic and copies ran while one was open for 3% -> 0% of each run, Pallas kernels for 6% -> 18%
where the time goes in v2:
time: 34.3 us; the launch traced here: 34.1 us
  starting transfers between devices  13.5 us (39%)
  Pallas kernels  11 us (32%)
  waiting for transfers between devices  9.33 us (27%)
    pallas_call x6, Pallas kernels, call(): pl.pallas_call(kernel, out_shape=out_shape, in_specs=specs, out_specs=jax...  9.47 us
    ppermute x3, starting transfers between devices, moved(): return lax.ppermute(value, ('tm', 'rows'), pairs)  7.57 us
    ppermute x3, starting transfers between devices, swapped(): return lax.ppermute(value, ('tm', 'rows'), pairs)  5.93 us
    ppermute x3, waiting for transfers between devices, swapped(): return lax.ppermute(value, ('tm', 'rows'), pairs)  5.11 us
    ppermute x3, waiting for transfers between devices, moved(): return lax.ppermute(value, ('tm', 'rows'), pairs)  4.22 us
    pallas_call x1, Pallas kernels, edge_rows(): pl.pallas_call(edge_kernel, out_shape=jax.ShapeDtypeStruct((cells.shape[0...  1.58 us
  transfers between devices with their start and end apart: 6, of which 5 were waited for; matrix products, arithmetic and copies ran while one was open for 0% of the time, Pallas kernels for 18%

profile of v2, /device:TPU:16, one launch (start us, length us, event | category | flops | bytes accessed | tf_op | source)
XLA Modules:
  0.0 34.1 jit_solution(9658793991220547210)
XLA Ops:
  0.0 0.0 copy-start.3
  0.0 0.0 copy-start.1
  0.0 2.0 %collective-permute-start = (bf16[2,8,128,128]{3,2,1,0:T(8,128)(2,1)}, bf16[2,8,128,128]{3,2,1,0:T(8,128)(2,1)S(1)}, u32[]{:S(2)}, u32[]{:S(2)}) collective-permute-start(bf16[2,8,128,128]{3,2,1,0:T(8,128)(2,1)} %frames.1), channel_id=1, source_target_pairs={{0,2},{1,3},{2,4},{3,5},{4,6},{5,7},{6,8},{7,9},{8,10},{9,11},{10,... | collective-permute-start | bytes 1572872 | tf_op jit(solution)/shard_map/ppermute | solution.py:22
  2.1 1.6 %shard_map.46 = bf16[2,2,128,128]{3,2,1,0:T(8,128)(2,1)} custom-call(bf16[2,8,128,128]{3,2,1,0:T(8,128)(2,1)} %frames.1), custom_call_target="tpu_custom_call" | custom-call | flops 4000000000 | bytes 1048576 | tf_op jit(solution)/shard_map/pallas_call | solution.py:40
  3.6 0.0 copy-start.2
  3.6 1.6 %collective-permute-start.2 = (bf16[2,2,128,128]{3,2,1,0:T(8,128)(2,1)}, bf16[2,2,128,128]{3,2,1,0:T(8,128)(2,1)S(1)}, u32[]{:S(2)}, u32[]{:S(2)}) collective-permute-start(bf16[2,2,128,128]{3,2,1,0:T(8,128)(2,1)} %shard_map.46), channel_id=1, source_target_pairs={{0,1},{1,0},{2,3},{3,2},{4,5},{5,4},{6,7},{7,6},{8,9},{9,8},{10,11... | collective-permute-start | bytes 393224 | tf_op jit(solution)/shard_map/ppermute | solution.py:28
  5.2 3.3 %collective-permute-start.1 = (bf16[2,2,128,128]{3,2,1,0:T(8,128)(2,1)}, bf16[2,2,128,128]{3,2,1,0:T(8,128)(2,1)S(1)}, u32[]{:S(2)}, u32[]{:S(2)}) collective-permute-start(bf16[2,2,128,128]{3,2,1,0:T(8,128)(2,1)} %shard_map.46), channel_id=1, source_target_pairs={{0,3},{1,2},{2,5},{3,4},{4,7},{5,6},{6,9},{7,8},{8,11},{9,10},{10,... | collective-permute-start | bytes 393224 | tf_op jit(solution)/shard_map/ppermute | solution.py:28
  8.6 0.1 add_convert_fusion.edges
  8.6 1.0 %collective-permute-done.2.above.below = bf16[2,2,128,128]{3,2,1,0:T(8,128)(2,1)S(1)} collective-permute-done((bf16[2,2,128,128]{3,2,1,0:T(8,128)(2,1)}, bf16[2,2,128,128]{3,2,1,0:T(8,128)(2,1)S(1)}, u32[]{:S(2)}, u32[]{:S(2)}) %collective-permute-start.2) | collective-permute-done | bytes 131104 | tf_op jit(solution)/shard_map/ppermute | solution.py:28
  9.7 0.0 copy-done.3
  9.7 0.0 copy-done.1
  9.7 2.1 %shard_map.47.own = f32[1152,256]{1,0:T(8,128)S(1)} custom-call(s32[2]{0:T(128)S(1)} %add_convert_fusion.edges, bf16[2,8,128,128]{3,2,1,0:T(8,128)(2,1)S(1)} %copy-done.3, bf16[2,2,128,128]{3,2,1,0:T(8,128)(2,1)S(1)} %collective-permute-done.2.above.below, bf16[2,2,128,128]{3,2,1,0:T(8,128)(2,1)S(1)} %collective-permute-done.2.above.below, ...), custom_call_target="tpu_custom_call" | custom-call | flops 1358954496 | bytes 1671176 | tf_op jit(solution)/shard_map/pallas_call | solution.py:206
  11.8 0.0 copy-start
  11.8 2.4 %collective-permute-done.1.above.below = bf16[2,2,128,128]{3,2,1,0:T(8,128)(2,1)S(1)} collective-permute-done((bf16[2,2,128,128]{3,2,1,0:T(8,128)(2,1)}, bf16[2,2,128,128]{3,2,1,0:T(8,128)(2,1)S(1)}, u32[]{:S(2)}, u32[]{:S(2)}) %collective-permute-start.1) | collective-permute-done | bytes 131104 | tf_op jit(solution)/shard_map/ppermute | solution.py:28
  14.2 0.0 collective-permute-done.frames
  14.2 0.0 copy-done.2
  14.2 3.0 %shard_map.48.field = bf16[1,4,64,256]{3,2,1,0:T(8,128)(2,1)S(1)} custom-call(s32[2]{0:T(128)S(1)} %add_convert_fusion.edges, bf16[2,8,128,128]{3,2,1,0:T(8,128)(2,1)S(1)} %collective-permute-done.frames, bf16[2,2,128,128]{3,2,1,0:T(8,128)(2,1)S(1)} %collective-permute-done.1.above.below, bf16[2,2,128,128]{3,2,1,0:T(8,128)(2,1)S(1)} %collective-permute-done.1.above.below, ...), custom_call_target="tpu_custom_call" | custom-call | flops 1358954496 | bytes 3440648 | tf_op jit(solution)/shard_map/pallas_call | solution.py:206
  17.2 2.1 %collective-permute-start.4 = (bf16[1,4,64,256]{3,2,1,0:T(8,128)(2,1)S(1)}, bf16[1,4,64,256]{3,2,1,0:T(8,128)(2,1)S(1)}, u32[]{:S(2)}, u32[]{:S(2)}) collective-permute-start(bf16[1,4,64,256]{3,2,1,0:T(8,128)(2,1)S(1)} %shard_map.48.field), channel_id=1, source_target_pairs={{0,2},{1,3},{2,4},{3,5},{4,6},{5,7},{6,8},{7,9},{8,10},{9,11},{10,... | collective-permute-start | bytes 393224 | tf_op jit(solution)/shard_map/ppermute | solution.py:22
  19.4 3.4 %collective-permute-start.3 = (bf16[1,4,64,256]{3,2,1,0:T(8,128)(2,1)S(1)}, bf16[1,4,64,256]{3,2,1,0:T(8,128)(2,1)S(1)}, u32[]{:S(2)}, u32[]{:S(2)}) collective-permute-start(bf16[1,4,64,256]{3,2,1,0:T(8,128)(2,1)S(1)} %shard_map.48.field), channel_id=1, source_target_pairs={{0,4},{1,5},{2,6},{3,7},{4,8},{5,9},{6,10},{7,11},{8,12},{9,13},{1... | collective-permute-start | bytes 393224 | tf_op jit(solution)/shard_map/ppermute | solution.py:22
  22.7 0.0 copy-done
  22.8 1.0 %shard_map.49 = (f32[256,256]{1,0:T(8,128)S(1)}, f32[1,64,256]{2,1,0:T(8,128)S(1)}) custom-call(s32[2]{0:T(128)S(1)} %add_convert_fusion.edges, bf16[1,4,64,256]{3,2,1,0:T(8,128)(2,1)S(1)} %shard_map.48.field, bf16[3,3,768,256]{3,2,1,0:T(8,128)(2,1)S(1)} %copy-done), custom_call_target="tpu_custom_call" | custom-call | flops 301989888 | bytes 3670024 | tf_op jit(solution)/shard_map/pallas_call | solution.py:206
  23.8 0.6 %collective-permute-done.4.field_1 = bf16[1,4,64,256]{3,2,1,0:T(8,128)(2,1)S(1)} collective-permute-done((bf16[1,4,64,256]{3,2,1,0:T(8,128)(2,1)S(1)}, bf16[1,4,64,256]{3,2,1,0:T(8,128)(2,1)S(1)}, u32[]{:S(2)}, u32[]{:S(2)}) %collective-permute-start.4) | collective-permute-done | bytes 131104 | tf_op jit(solution)/shard_map/ppermute | solution.py:22
  24.4 3.6 %collective-permute-done.3.field_0 = bf16[1,4,64,256]{3,2,1,0:T(8,128)(2,1)S(1)} collective-permute-done((bf16[1,4,64,256]{3,2,1,0:T(8,128)(2,1)S(1)}, bf16[1,4,64,256]{3,2,1,0:T(8,128)(2,1)S(1)}, u32[]{:S(2)}, u32[]{:S(2)}) %collective-permute-start.3) | collective-permute-done | bytes 131104 | tf_op jit(solution)/shard_map/ppermute | solution.py:22
  28.0 0.8 %shard_map.51 = bf16[1,64,256]{2,1,0:T(8,128)(2,1)S(1)} custom-call(s32[2]{0:T(128)S(1)} %add_convert_fusion.edges, bf16[1,4,64,256]{3,2,1,0:T(8,128)(2,1)S(1)} %collective-permute-done.3.field_0, bf16[1,4,64,256]{3,2,1,0:T(8,128)(2,1)S(1)} %collective-permute-done.4.field_1, bf16[3,3,768,256]{3,2,1,0:T(8,128)(2,1)S(1)} %copy-done, ...), custom_call_target="tpu_custom_call" | custom-call | flops 75497472 | bytes 3866632 | tf_op jit(solution)/shard_map/pallas_call | solution.py:206
  28.8 1.0 %collective-permute-start.5 = (bf16[1,64,256]{2,1,0:T(8,128)(2,1)S(1)}, bf16[1,64,256]{2,1,0:T(8,128)(2,1)S(1)}, u32[]{:S(2)}, u32[]{:S(2)}) collective-permute-start(bf16[1,64,256]{2,1,0:T(8,128)(2,1)S(1)} %shard_map.51), channel_id=1, source_target_pairs={{0,1},{1,0},{2,3},{3,2},{4,5},{5,4},{6,7},{7,6},{8,9},{9,8},{10,11... | collective-permute-start | bytes 98312 | tf_op jit(solution)/shard_map/ppermute | solution.py:28
  29.8 1.2 %shard_map.50.total = f32[256,256]{1,0:T(8,128)S(1)} custom-call(s32[2]{0:T(128)S(1)} %add_convert_fusion.edges, bf16[1,4,64,256]{3,2,1,0:T(8,128)(2,1)S(1)} %collective-permute-done.3.field_0, bf16[1,4,64,256]{3,2,1,0:T(8,128)(2,1)S(1)} %collective-permute-done.4.field_1, bf16[3,3,768,256]{3,2,1,0:T(8,128)(2,1)S(1)} %copy-done, ...), custom_call_target="tpu_custom_call" | custom-call | flops 603979776 | bytes 4063240 | tf_op jit(solution)/shard_map/pallas_call | solution.py:206
  31.1 1.7 %collective-permute-done.5.above.below = bf16[1,64,256]{2,1,0:T(8,128)(2,1)S(1)} collective-permute-done((bf16[1,64,256]{2,1,0:T(8,128)(2,1)S(1)}, bf16[1,64,256]{2,1,0:T(8,128)(2,1)S(1)}, u32[]{:S(2)}, u32[]{:S(2)}) %collective-permute-start.5) | collective-permute-done | bytes 32800 | tf_op jit(solution)/shard_map/ppermute | solution.py:28
  32.8 1.3 %shard_map.52 = bf16[1,4,64,256]{3,2,1,0:T(8,128)(2,1)} custom-call(s32[2]{0:T(128)S(1)} %add_convert_fusion.edges, f32[256,256]{1,0:T(8,128)S(1)} %shard_map.50.total, bf16[1,64,256]{2,1,0:T(8,128)(2,1)S(1)} %collective-permute-done.5.above.below, bf16[1,64,256]{2,1,0:T(8,128)(2,1)S(1)} %collective-permute-done.5.above.below), custom_call_target="tpu_custom_call" | custom-call | flops 65536 | bytes 327688 | tf_op jit(solution)/shard_map/pallas_call | solution.py:206
Async XLA Ops:
  0.0 9.7 %copy-start.3 = (bf16[2,8,128,128]{3,2,1,0:T(8,128)(2,1)S(1)}, bf16[2,8,128,128]{3,2,1,0:T(8,128)(2,1)}, u32[]{:S(2)}) copy-start(bf16[2,8,128,128]{3,2,1,0:T(8,128)(2,1)} %frames.1) | copy-start | bytes 1572868
  0.0 9.7 %copy-start.1 = (bf16[3,3,384,128]{3,2,1,0:T(8,128)(2,1)S(1)}, bf16[3,3,384,128]{3,2,1,0:T(8,128)(2,1)}, u32[]{:S(2)}) copy-start(bf16[3,3,384,128]{3,2,1,0:T(8,128)(2,1)} %weight.6) | copy-start | bytes 2654212
  0.0 14.2 %collective-permute-start = (bf16[2,8,128,128]{3,2,1,0:T(8,128)(2,1)}, bf16[2,8,128,128]{3,2,1,0:T(8,128)(2,1)S(1)}, u32[]{:S(2)}, u32[]{:S(2)}) collective-permute-start(bf16[2,8,128,128]{3,2,1,0:T(8,128)(2,1)} %frames.1), channel_id=1, source_target_pairs={{0,2},{1,3},{2,4},{3,5},{4,6},{5,7},{6,8},{7,9},{8,10},{9,11},{10,... | collective-permute-start | bytes 1572872 | tf_op jit(solution)/shard_map/ppermute | solution.py:22
  3.6 10.6 %copy-start.2 = (bf16[3,384,256]{2,1,0:T(8,128)(2,1)S(1)}, bf16[3,384,256]{2,1,0:T(8,128)(2,1)}, u32[]{:S(2)}) copy-start(bf16[3,384,256]{2,1,0:T(8,128)(2,1)} %down.1) | copy-start | bytes 1769476
  3.6 6.0 %collective-permute-start.2 = (bf16[2,2,128,128]{3,2,1,0:T(8,128)(2,1)}, bf16[2,2,128,128]{3,2,1,0:T(8,128)(2,1)S(1)}, u32[]{:S(2)}, u32[]{:S(2)}) collective-permute-start(bf16[2,2,128,128]{3,2,1,0:T(8,128)(2,1)} %shard_map.46), channel_id=1, source_target_pairs={{0,1},{1,0},{2,3},{3,2},{4,5},{5,4},{6,7},{7,6},{8,9},{9,8},{10,11... | collective-permute-start | bytes 393224 | tf_op jit(solution)/shard_map/ppermute | solution.py:28
  5.2 9.0 %collective-permute-start.1 = (bf16[2,2,128,128]{3,2,1,0:T(8,128)(2,1)}, bf16[2,2,128,128]{3,2,1,0:T(8,128)(2,1)S(1)}, u32[]{:S(2)}, u32[]{:S(2)}) collective-permute-start(bf16[2,2,128,128]{3,2,1,0:T(8,128)(2,1)} %shard_map.46), channel_id=1, source_target_pairs={{0,3},{1,2},{2,5},{3,4},{4,7},{5,6},{6,9},{7,8},{8,11},{9,10},{10,... | collective-permute-start | bytes 393224 | tf_op jit(solution)/shard_map/ppermute | solution.py:28
  11.8 10.9 %copy-start = (bf16[3,3,768,256]{3,2,1,0:T(8,128)(2,1)S(1)}, bf16[3,3,768,256]{3,2,1,0:T(8,128)(2,1)}, u32[]{:S(2)}) copy-start(bf16[3,3,768,256]{3,2,1,0:T(8,128)(2,1)} %weight.9) | copy-start | bytes 10616836
  17.2 7.2 %collective-permute-start.4 = (bf16[1,4,64,256]{3,2,1,0:T(8,128)(2,1)S(1)}, bf16[1,4,64,256]{3,2,1,0:T(8,128)(2,1)S(1)}, u32[]{:S(2)}, u32[]{:S(2)}) collective-permute-start(bf16[1,4,64,256]{3,2,1,0:T(8,128)(2,1)S(1)} %shard_map.48.field), channel_id=1, source_target_pairs={{0,2},{1,3},{2,4},{3,5},{4,6},{5,7},{6,8},{7,9},{8,10},{9,11},{10,... | collective-permute-start | bytes 393224 | tf_op jit(solution)/shard_map/ppermute | solution.py:22
  19.4 8.7 %collective-permute-start.3 = (bf16[1,4,64,256]{3,2,1,0:T(8,128)(2,1)S(1)}, bf16[1,4,64,256]{3,2,1,0:T(8,128)(2,1)S(1)}, u32[]{:S(2)}, u32[]{:S(2)}) collective-permute-start(bf16[1,4,64,256]{3,2,1,0:T(8,128)(2,1)S(1)} %shard_map.48.field), channel_id=1, source_target_pairs={{0,4},{1,5},{2,6},{3,7},{4,8},{5,9},{6,10},{7,11},{8,12},{9,13},{1... | collective-permute-start | bytes 393224 | tf_op jit(solution)/shard_map/ppermute | solution.py:22
  28.8 4.0 %collective-permute-start.5 = (bf16[1,64,256]{2,1,0:T(8,128)(2,1)S(1)}, bf16[1,64,256]{2,1,0:T(8,128)(2,1)S(1)}, u32[]{:S(2)}, u32[]{:S(2)}) collective-permute-start(bf16[1,64,256]{2,1,0:T(8,128)(2,1)S(1)} %shard_map.51), channel_id=1, source_target_pairs={{0,1},{1,0},{2,3},{3,2},{4,5},{5,4},{6,7},{7,6},{8,9},{9,8},{10,11... | collective-permute-start | bytes 98312 | tf_op jit(solution)/shard_map/ppermute | solution.py:28

commit v3 on v2

v3 whole, which is shorter than its diff:
```python
import functools

import jax
import jax.numpy as jnp
from jax import lax
from jax.experimental import pallas as pl
from jax.experimental.pallas import tpu as pltpu
from jax.sharding import PartitionSpec as P

F32 = jnp.float32
BF16 = jnp.bfloat16


def moved(value, steps, hop):
    tm, rows = lax.axis_size("tm"), lax.axis_size("rows")
    pairs = [
        (t * rows + r, (t + steps) * rows + r + hop)
        for t in range(tm - steps)
        for r in range(rows)
        if 0 <= r + hop < rows
    ]
    return lax.ppermute(value, ("tm", "rows"), pairs)


def swapped(value, steps):
    tm = lax.axis_size("tm")
    pairs = [(t * 2 + r, (t + steps) * 2 + 1 - r) for t in range(tm - steps) for r in range(2)]
    return lax.ppermute(value, ("tm", "rows"), pairs)


def paired(value, step):
    tm, rows = lax.axis_size("tm"), lax.axis_size("rows")
    start = 0 if step > 0 else 1
    pairs = [(t * rows + r, (t + step) * rows + r) for t in range(start, tm, 2) for r in range(rows)]
    return lax.ppermute(value, ("tm", "rows"), pairs)


def place_kernel(out):
    strip = lax.axis_index("rows")
    out[0] = (strip > 0).astype(jnp.int32)
    out[1] = (strip < lax.axis_size("rows") - 1).astype(jnp.int32)
    out[2] = lax.axis_index("tm") % 2


def edge_kernel(edges, cells, out):
    width = out.shape[1]
    out[...] = cells[:, pl.ds(edges[1] * (cells.shape[1] - width), width)]


def frame_rims(edges, frames):
    rows = frames.shape[1]
    if lax.axis_size("rows") == 2:
        sent = call(
            edge_kernel,
            jax.ShapeDtypeStruct((frames.shape[0], 2, *frames.shape[2:]), BF16),
            [],
            0,
            (edges, frames),
        )
        return [(both, both) for both in (swapped(sent, 0), swapped(sent, 1))]
    head, tail = frames[:, :2], frames[:, rows - 1 :]
    return [(moved(tail, steps, 1), moved(head, steps, -1)) for steps in (0, 1)]


def column_shift(value, cols, steps):
    size = value.shape[0]
    column = lax.broadcasted_iota(jnp.int32, value.shape, 0) % cols
    edge = 0 if steps > 0 else cols - 1
    return jnp.where(column == edge, 0.0, pltpu.roll(value, steps % size, 0))


def shifted_columns(flat, cols):
    wide = flat.astype(F32)
    return column_shift(wide, cols, 1).astype(BF16), column_shift(wide, cols, -1).astype(BF16)


def tap_matrix(weight, first_tap, row_taps, e, channels):
    zero = jnp.zeros((channels, channels), BF16)

    def pick(tap, b):
        return weight[tap, b, e * channels : (e + 1) * channels] if 0 <= tap <= 2 else zero

    return jnp.concatenate(
        [
            jnp.concatenate([pick(first_tap + f, b), pick(first_tap + f - 1, b)], axis=1)
            for f in range(2)
            for b in row_taps
        ],
        axis=0,
    )


def fine_rows(row, outs, row_taps, weight, first_tap):
    channels = weight.shape[-1]
    some = next(x for f in range(2) for r in outs for b in row_taps if (x := row(f, r - 1 + b)) is not None)
    cols = some.shape[0]
    zero = jnp.zeros((cols, channels), BF16)

    def cell(f, i):
        found = row(f, i)
        return zero if found is None else found

    left = jnp.concatenate(
        [
            jnp.concatenate([cell(f, r - 1 + b) for f in range(2) for b in row_taps], axis=1)
            for r in outs
        ],
        axis=0,
    )
    sums = [
        jnp.dot(
            left, tap_matrix(weight, first_tap, row_taps, e, channels), preferred_element_type=F32
        )
        for e in range(3)
    ]
    return sums[1] + column_shift(sums[0], cols, 1) + column_shift(sums[2], cols, -1)


def chunks_of(count):
    size = next(c for c in (3, 2, 1) if count % c == 0)
    return [range(i, i + size) for i in range(0, count, size)]


def fine_own_kernel(frames, weight, out):
    _, rows, cols, _ = frames.shape

    def row(f, i):
        return frames[f, i] if 0 <= i < rows else None

    for outs in chunks_of(rows + 1):
        out[outs[0] * cols : (outs[-1] + 1) * cols] = fine_rows(row, outs, range(3), weight, 2)


def halo_row(edges, above, below, rows):
    def row(f, i):
        if i == -1:
            cells, have = above[f, above.shape[1] - 1], edges[0]
        elif i >= rows:
            cells, have = below[f, i - rows], edges[1]
        else:
            return None
        return jnp.where(have != 0, cells, jnp.zeros_like(cells))

    return row


def fine_halo_kernel(edges, above, below, weight, out, *, rows):
    cols = above.shape[2]
    row = halo_row(edges, above, below, rows)
    out[:cols] = fine_rows(row, [0], [0], weight, 2)
    out[cols:] = fine_rows(row, [rows - 1, rows], [1, 2], weight, 2)


def silu(v):
    return v / (1.0 + jnp.exp(-v))


def fine_rest_kernel(edges, frames, above, below, weight, own, halo, down, out, pooled):
    _, rows, cols, channels = frames.shape
    outside = halo_row(edges, above, below, rows)

    def row(f, i):
        return frames[f, i] if 0 <= i < rows else outside(f, i)

    pad = pooled.shape[1] - cols
    pooled[:, cols:] = jnp.zeros((rows + 1, pad, channels), F32)
    for outs in chunks_of(rows + 1):
        total = fine_rows(row, outs, range(3), weight, 0)
        for i, r in enumerate(outs):
            line = total[i * cols : (i + 1) * cols] + own[r * cols : (r + 1) * cols]
            for k, halo_r in enumerate((0, rows - 1, rows)):
                if r == halo_r:
                    line = line + halo[k * cols : (k + 1) * cols]
            fine = silu(line).astype(BF16).astype(F32)
            mean = ((fine[:, :channels] + fine[:, channels:]) * 0.5).astype(BF16).astype(F32)
            if r == rows:
                mean = jnp.where(edges[1] != 0, mean, 0.0)
            pooled[r, :cols] = mean
    strips = []
    for p in range(rows // 2):
        pieces = [
            pooled[2 * p + b, pl.ds(e, cols // 2, stride=2), :].astype(BF16)
            for b in range(3)
            for e in range(3)
        ]
        strips.append(jnp.concatenate(pieces, axis=1))
    left = jnp.concatenate(strips, axis=0)
    right = down[...].reshape(-1, down.shape[-1])
    out[...] = jnp.dot(left, right, preferred_element_type=F32).astype(BF16).reshape(out.shape)


def field_taps(field):
    _, rows, cols, channels = field.shape
    flat = field[0].reshape(rows * cols, channels)
    left, right = shifted_columns(flat, cols)
    return jnp.concatenate([left, flat, right], axis=1)


def rim_sum(edges, taps, weight, a, cols, both):
    size = taps.shape[0]
    dot = functools.partial(jnp.dot, preferred_element_type=F32)
    if both:
        return [dot(taps[:cols], weight[a, 2]), dot(taps[size - cols :], weight[a, 0])]
    row = jnp.where(edges[0] != 0, taps[:cols], taps[size - cols :])
    return [dot(row, weight[a, 2 * edges[0]])]


def body_sum(taps, weight, a, cols):
    size = taps.shape[0]
    dot = functools.partial(jnp.dot, preferred_element_type=F32)
    zero = jnp.zeros((cols, weight.shape[-1]), F32)
    upper = jnp.concatenate([zero, dot(taps[: size - cols], weight[a, 0])], axis=0)
    lower = jnp.concatenate([dot(taps[cols:], weight[a, 2]), zero], axis=0)
    return dot(taps, weight[a, 1]) + upper + lower


def coarse_first_kernel(edges, field, weight, body, rim):
    taps = field_taps(field)
    cols = field.shape[2]
    body[...] = body_sum(taps, weight, 2, cols)
    for i, part in enumerate(rim_sum(edges, taps, weight, 2, cols, rim.shape[0] == 2)):
        rim[i] = part


def coarse_next_kernel(edges, field, weight, body_in, rim_in, body, rim):
    taps = field_taps(field)
    cols = field.shape[2]
    body[...] = body_in[...] + body_sum(taps, weight, 0, cols)
    for i, part in enumerate(rim_sum(edges, taps, weight, 0, cols, rim.shape[0] == 2)):
        rim[i] = rim_in[i] + part


def middle_taps(edges, direct, relayed):
    field = jnp.where(edges[2] != 0, direct[...], relayed[...])
    return field_taps(field)


def coarse_rim_kernel(edges, direct, relayed, weight, rim, out):
    cols = direct.shape[2]
    taps = middle_taps(edges, direct, relayed)
    for i, part in enumerate(rim_sum(edges, taps, weight, 1, cols, rim.shape[0] == 2)):
        out[i] = (rim[i] + part).astype(BF16)


def coarse_last_kernel(edges, direct, relayed, weight, body, out):
    cols = direct.shape[2]
    taps = middle_taps(edges, direct, relayed)
    out[...] = body[...] + body_sum(taps, weight, 1, cols)


def finish_kernel(edges, total, above, below, out):
    _, rows, cols, channels = out.shape
    for p in range(rows):
        row = total[p * cols : (p + 1) * cols]
        if p == 0:
            row = row + jnp.where(edges[0] != 0, above[0].astype(F32), 0.0)
        if p == rows - 1:
            row = row + jnp.where(edges[1] != 0, below[0].astype(F32), 0.0)
        out[0, p] = silu(row).astype(BF16)


def call(kernel, out_shape, scratch, flops, args):
    size = sum(a.size * a.dtype.itemsize for a in args)
    specs = [
        pl.BlockSpec(memory_space=pltpu.SMEM if a.ndim == 1 else pltpu.VMEM) for a in args
    ]
    return pl.pallas_call(
        kernel,
        out_shape=out_shape,
        in_specs=specs,
        out_specs=jax.tree.map(lambda _: pl.BlockSpec(memory_space=pltpu.VMEM), out_shape),
        scratch_shapes=scratch,
        cost_estimate=pl.CostEstimate(flops=flops, bytes_accessed=size, transcendentals=0),
        compiler_params=pltpu.CompilerParams(vmem_limit_bytes=20 * 1024 * 1024),
    )(*args)


def local(frames, conv_fine, conv_down, conv_coarse):
    _, rows, cols, channels = frames.shape
    wide = conv_down.shape[-1]
    strips, times = lax.axis_size("rows"), lax.axis_size("tm")
    edges = pl.pallas_call(
        place_kernel,
        out_shape=jax.ShapeDtypeStruct((3,), jnp.int32),
        out_specs=pl.BlockSpec(memory_space=pltpu.SMEM),
        cost_estimate=pl.CostEstimate(flops=4 * 10**9, bytes_accessed=1 << 20, transcendentals=0),
        compiler_params=pltpu.CompilerParams(vmem_limit_bytes=1024 * 1024),
    )()

    earlier = moved(frames, 1, 0)
    (above, below), (above_1, below_1) = frame_rims(edges, frames)
    size = (rows + 1) * cols
    pair = jax.ShapeDtypeStruct((size, 2 * channels), F32)
    flops = 2 * size * 18 * channels * 2 * channels
    own = call(fine_own_kernel, pair, [], flops, (frames, conv_fine))
    halo = call(
        functools.partial(fine_halo_kernel, rows=rows),
        jax.ShapeDtypeStruct((3 * cols, 2 * channels), F32),
        [],
        flops // 3,
        (edges, above, below, conv_fine),
    )
    half_rows, half_cols = rows // 2, cols // 2
    shape = jax.ShapeDtypeStruct((1, half_rows, half_cols, wide), BF16)
    field = call(
        fine_rest_kernel,
        shape,
        [pltpu.VMEM((rows + 1, cols + 8, channels), F32)],
        flops,
        (edges, earlier, above_1, below_1, conv_fine, own, halo, conv_down),
    )
    sides = 1 if strips == 2 else 2
    sums = jax.ShapeDtypeStruct((half_rows * half_cols, wide), F32)
    rims = jax.ShapeDtypeStruct((sides, half_cols, wide), F32)
    flops = 2 * half_rows * half_cols * 9 * wide * wide
    field_2 = moved(field, 2, 0)
    body, rim = call(coarse_first_kernel, (sums, rims), [], flops, (edges, field, conv_coarse))
    field_2, body, rim = lax.optimization_barrier((field_2, body, rim))
    if times % 2 == 0:
        direct = paired(field, 1)
        relayed = paired(field_2, -1)
    else:
        direct = relayed = moved(field, 1, 0)
    body, rim = call(
        coarse_next_kernel, (sums, rims), [], flops, (edges, field_2, conv_coarse, body, rim)
    )
    rim = call(
        coarse_rim_kernel,
        jax.ShapeDtypeStruct(rims.shape, BF16),
        [],
        flops // 4,
        (edges, direct, relayed, conv_coarse, rim),
    )
    if sides == 1:
        from_above = from_below = swapped(rim, 0)
    else:
        from_above, from_below = moved(rim[1:], 0, 1), moved(rim[:1], 0, -1)
    total = call(coarse_last_kernel, sums, [], flops, (edges, direct, relayed, conv_coarse, body))
    return call(finish_kernel, shape, [], sums.size, (edges, total, from_above, from_below))


def solution(mesh):
    placed = (P("tm", "rows", None, None), P(), P(), P())
    return jax.shard_map(
        local, mesh=mesh, in_specs=placed, out_specs=P("tm", "rows", None, None), check_vma=False
    )
```

time: 34.3 us -> 34.1 us (level)
  waiting for transfers between devices: 9.33 us -> 8.56 us
  Pallas kernels: 11 us -> 11.5 us
    ppermute x0 -> x2, starting transfers between devices: none -> 3.51 us  [paired(): return lax.ppermute(value, ('tm', 'rows'), pairs)]
    ppermute x3 -> x2, starting transfers between devices: 7.57 us -> 4.64 us  [moved(): return lax.ppermute(value, ('tm', 'rows'), pairs)]
    ppermute x3 -> x2, waiting for transfers between devices: 4.22 us -> 1.88 us  [moved(): return lax.ppermute(value, ('tm', 'rows'), pairs)]
    pallas_call x6 -> x9, Pallas kernels: 9.47 us -> 10.9 us  [call(): pl.pallas_call(kernel, out_shape=out_shape, in_specs=specs, out_specs=jax...]
    pallas_call x1, Pallas kernels: 1.58 us -> 0.61 us  [local(): pl.pallas_call(place_kernel, out_shape=jax.ShapeDtypeStruct((3,), jnp.int...]
    ppermute x0 -> x2, waiting for transfers between devices: none -> 0.9 us  [paired(): return lax.ppermute(value, ('tm', 'rows'), pairs)]
    ppermute x3, waiting for transfers between devices: 5.11 us -> 5.78 us  [swapped(): return lax.ppermute(value, ('tm', 'rows'), pairs)]
    ppermute x3, starting transfers between devices: 5.93 us -> 5.48 us  [swapped(): return lax.ppermute(value, ('tm', 'rows'), pairs)]
  transfers between devices with their start and end apart: 6 -> 7, of which waited for: 5 -> 4; matrix products, arithmetic and copies ran while one was open for 0% -> 0% of each run, Pallas kernels for 18% -> 20%
where the time goes in v3:
time: 34.1 us; the launch traced here: 33.9 us
  starting transfers between devices  13.6 us (40%)
  Pallas kernels  11.5 us (34%)
  waiting for transfers between devices  8.56 us (25%)
    pallas_call x9, Pallas kernels, call(): pl.pallas_call(kernel, out_shape=out_shape, in_specs=specs, out_specs=jax...  10.9 us
    ppermute x3, waiting for transfers between devices, swapped(): return lax.ppermute(value, ('tm', 'rows'), pairs)  5.78 us
    ppermute x3, starting transfers between devices, swapped(): return lax.ppermute(value, ('tm', 'rows'), pairs)  5.48 us
    ppermute x2, starting transfers between devices, moved(): return lax.ppermute(value, ('tm', 'rows'), pairs)  4.64 us
    ppermute x2, starting transfers between devices, paired(): return lax.ppermute(value, ('tm', 'rows'), pairs)  3.51 us
    ppermute x2, waiting for transfers between devices, moved(): return lax.ppermute(value, ('tm', 'rows'), pairs)  1.88 us
    ppermute x2, waiting for transfers between devices, paired(): return lax.ppermute(value, ('tm', 'rows'), pairs)  0.9 us
  transfers between devices with their start and end apart: 7, of which 4 were waited for; matrix products, arithmetic and copies ran while one was open for 0% of the time, Pallas kernels for 20%

profile of v3, /device:TPU:16, one launch (start us, length us, event | category | flops | bytes accessed | tf_op | source)
XLA Modules:
  0.0 33.9 jit_solution(4152077056608906846)
XLA Ops:
  0.0 0.0 copy-start.1
  0.0 0.0 copy-start.2
  0.0 2.0 %collective-permute-start = (bf16[2,8,128,128]{3,2,1,0:T(8,128)(2,1)}, bf16[2,8,128,128]{3,2,1,0:T(8,128)(2,1)S(1)}, u32[]{:S(2)}, u32[]{:S(2)}) collective-permute-start(bf16[2,8,128,128]{3,2,1,0:T(8,128)(2,1)} %frames.1), channel_id=1, source_target_pairs={{0,2},{1,3},{2,4},{3,5},{4,6},{5,7},{6,8},{7,9},{8,10},{9,11},{10,... | collective-permute-start | bytes 1572872 | tf_op jit(solution)/shard_map/ppermute | solution.py:22
  2.1 0.6 %shard_map.46.edges = s32[3]{0:T(128)S(1)} custom-call(), custom_call_target="tpu_custom_call" | custom-call | flops 4000000000 | bytes 1048576 | tf_op jit(solution)/shard_map/pallas_call | solution.py:282
  2.7 0.0 copy-done.1
  2.7 0.0 copy-start.3
  2.7 0.6 %shard_map.47 = bf16[2,2,128,128]{3,2,1,0:T(8,128)(2,1)S(1)} custom-call(s32[3]{0:T(128)S(1)} %shard_map.46.edges, bf16[2,8,128,128]{3,2,1,0:T(8,128)(2,1)S(1)} %copy-done.1), custom_call_target="tpu_custom_call" | custom-call | bytes 524300 | tf_op jit(solution)/shard_map/pallas_call | solution.py:267
  3.3 1.6 %collective-permute-start.2 = (bf16[2,2,128,128]{3,2,1,0:T(8,128)(2,1)S(1)}, bf16[2,2,128,128]{3,2,1,0:T(8,128)(2,1)S(1)}, u32[]{:S(2)}, u32[]{:S(2)}) collective-permute-start(bf16[2,2,128,128]{3,2,1,0:T(8,128)(2,1)S(1)} %shard_map.47), channel_id=1, source_target_pairs={{0,1},{1,0},{2,3},{3,2},{4,5},{5,4},{6,7},{7,6},{8,9},{9,8},{10,11... | collective-permute-start | bytes 393224 | tf_op jit(solution)/shard_map/ppermute | solution.py:28
  4.8 3.3 %collective-permute-start.1 = (bf16[2,2,128,128]{3,2,1,0:T(8,128)(2,1)S(1)}, bf16[2,2,128,128]{3,2,1,0:T(8,128)(2,1)S(1)}, u32[]{:S(2)}, u32[]{:S(2)}) collective-permute-start(bf16[2,2,128,128]{3,2,1,0:T(8,128)(2,1)S(1)} %shard_map.47), channel_id=1, source_target_pairs={{0,3},{1,2},{2,5},{3,4},{4,7},{5,6},{6,9},{7,8},{8,11},{9,10},{10,... | collective-permute-start | bytes 393224 | tf_op jit(solution)/shard_map/ppermute | solution.py:28
  8.2 0.0 copy-done.2
  8.2 1.6 %shard_map.48.own = f32[1152,256]{1,0:T(8,128)S(1)} custom-call(bf16[2,8,128,128]{3,2,1,0:T(8,128)(2,1)S(1)} %copy-done.1, bf16[3,3,384,128]{3,2,1,0:T(8,128)(2,1)S(1)} %copy-done.2), custom_call_target="tpu_custom_call" | custom-call | flops 1358954496 | bytes 1409024 | tf_op jit(solution)/shard_map/pallas_call | solution.py:267
  9.7 0.0 copy-start
  9.8 0.0 collective-permute-done.2.above.below
  9.8 1.0 %shard_map.49.halo = f32[384,256]{1,0:T(8,128)S(1)} custom-call(s32[3]{0:T(128)S(1)} %shard_map.46.edges, bf16[2,2,128,128]{3,2,1,0:T(8,128)(2,1)S(1)} %collective-permute-done.2.above.below, bf16[2,2,128,128]{3,2,1,0:T(8,128)(2,1)S(1)} %collective-permute-done.2.above.below, bf16[3,3,384,128]{3,2,1,0:T(8,128)(2,1)S(1)} %copy-done.2), custom_call_target="tpu_custom_call" | custom-call | flops 452984832 | bytes 1146892 | tf_op jit(solution)/shard_map/pallas_call | solution.py:267
  10.7 3.4 %collective-permute-done.1.above.below = bf16[2,2,128,128]{3,2,1,0:T(8,128)(2,1)S(1)} collective-permute-done((bf16[2,2,128,128]{3,2,1,0:T(8,128)(2,1)S(1)}, bf16[2,2,128,128]{3,2,1,0:T(8,128)(2,1)S(1)}, u32[]{:S(2)}, u32[]{:S(2)}) %collective-permute-start.1) | collective-permute-done | bytes 131104 | tf_op jit(solution)/shard_map/ppermute | solution.py:28
  14.1 0.0 collective-permute-done.frames
  14.1 0.0 copy-done.3
  14.1 2.8 %shard_map.50.field = bf16[1,4,64,256]{3,2,1,0:T(8,128)(2,1)S(1)} custom-call(s32[3]{0:T(128)S(1)} %shard_map.46.edges, bf16[2,8,128,128]{3,2,1,0:T(8,128)(2,1)S(1)} %collective-permute-done.frames, bf16[2,2,128,128]{3,2,1,0:T(8,128)(2,1)S(1)} %collective-permute-done.1.above.below, bf16[2,2,128,128]{3,2,1,0:T(8,128)(2,1)S(1)} %collective-permute-done.1.above.below, ...), custom_call_target="tpu_custom_call" | custom-call | flops 1358954496 | bytes 3833868 | tf_op jit(solution)/shard_map/pallas_call | solution.py:267
  16.9 2.6 %collective-permute-start.4 = (bf16[1,4,64,256]{3,2,1,0:T(8,128)(2,1)S(1)}, bf16[1,4,64,256]{3,2,1,0:T(8,128)(2,1)S(1)}, u32[]{:S(2)}, u32[]{:S(2)}) collective-permute-start(bf16[1,4,64,256]{3,2,1,0:T(8,128)(2,1)S(1)} %shard_map.50.field), channel_id=1, source_target_pairs={{0,4},{1,5},{2,6},{3,7},{4,8},{5,9},{6,10},{7,11},{8,12},{9,13},{1... | collective-permute-start | bytes 393224 | tf_op jit(solution)/shard_map/ppermute | solution.py:22
  19.5 2.2 %collective-permute-start.3 = (bf16[1,4,64,256]{3,2,1,0:T(8,128)(2,1)S(1)}, bf16[1,4,64,256]{3,2,1,0:T(8,128)(2,1)S(1)}, u32[]{:S(2)}, u32[]{:S(2)}) collective-permute-start(bf16[1,4,64,256]{3,2,1,0:T(8,128)(2,1)S(1)} %shard_map.50.field), channel_id=1, source_target_pairs={{0,2},{1,3},{4,6},{5,7},{8,10},{9,11},{12,14},{13,15},{16,18},{17,... | collective-permute-start | bytes 393224 | tf_op jit(solution)/shard_map/ppermute | solution.py:35
  21.7 0.0 copy-done
  21.7 1.0 %shard_map.51 = (f32[256,256]{1,0:T(8,128)S(1)}, f32[1,64,256]{2,1,0:T(8,128)S(1)}) custom-call(s32[3]{0:T(128)S(1)} %shard_map.46.edges, bf16[1,4,64,256]{3,2,1,0:T(8,128)(2,1)S(1)} %shard_map.50.field, bf16[3,3,768,256]{3,2,1,0:T(8,128)(2,1)S(1)} %copy-done), custom_call_target="tpu_custom_call" | custom-call | flops 301989888 | bytes 3670028 | tf_op jit(solution)/shard_map/pallas_call | solution.py:267
  22.8 1.9 %collective-permute-done.4.field = bf16[1,4,64,256]{3,2,1,0:T(8,128)(2,1)S(1)} collective-permute-done((bf16[1,4,64,256]{3,2,1,0:T(8,128)(2,1)S(1)}, bf16[1,4,64,256]{3,2,1,0:T(8,128)(2,1)S(1)}, u32[]{:S(2)}, u32[]{:S(2)}) %collective-permute-start.4) | collective-permute-done | bytes 131104 | tf_op jit(solution)/shard_map/ppermute | solution.py:22
  24.6 1.3 %collective-permute-start.5 = (bf16[1,4,64,256]{3,2,1,0:T(8,128)(2,1)S(1)}, bf16[1,4,64,256]{3,2,1,0:T(8,128)(2,1)S(1)}, u32[]{:S(2)}, u32[]{:S(2)}) collective-permute-start(bf16[1,4,64,256]{3,2,1,0:T(8,128)(2,1)S(1)} %collective-permute-done.4.field), channel_id=1, source_target_pairs={{2,0},{3,1},{6,4},{7,5},{10,8},{11,9},{14,12},{15,13},{18,16},{19,... | collective-permute-start | bytes 393224 | tf_op jit(solution)/shard_map/ppermute | solution.py:35
  25.9 1.0 %shard_map.52 = (f32[256,256]{1,0:T(8,128)S(1)}, f32[1,64,256]{2,1,0:T(8,128)S(1)}) custom-call(s32[3]{0:T(128)S(1)} %shard_map.46.edges, bf16[1,4,64,256]{3,2,1,0:T(8,128)(2,1)S(1)} %collective-permute-done.4.field, bf16[3,3,768,256]{3,2,1,0:T(8,128)(2,1)S(1)} %copy-done, f32[256,256]{1,0:T(8,128)S(1)} %get-tuple-element.15.body_in, ...), custom_call_target="tpu_custom_call" | custom-call | flops 301989888 | bytes 3997708 | tf_op jit(solution)/shard_map/pallas_call | solution.py:267
  27.0 0.0 collective-permute-done.3.direct
  27.0 0.9 %collective-permute-done.5.relayed = bf16[1,4,64,256]{3,2,1,0:T(8,128)(2,1)S(1)} collective-permute-done((bf16[1,4,64,256]{3,2,1,0:T(8,128)(2,1)S(1)}, bf16[1,4,64,256]{3,2,1,0:T(8,128)(2,1)S(1)}, u32[]{:S(2)}, u32[]{:S(2)}) %collective-permute-start.5) | collective-permute-done | bytes 131104 | tf_op jit(solution)/shard_map/ppermute | solution.py:35
  27.9 0.7 %shard_map.54 = bf16[1,64,256]{2,1,0:T(8,128)(2,1)S(1)} custom-call(s32[3]{0:T(128)S(1)} %shard_map.46.edges, bf16[1,4,64,256]{3,2,1,0:T(8,128)(2,1)S(1)} %collective-permute-done.3.direct, bf16[1,4,64,256]{3,2,1,0:T(8,128)(2,1)S(1)} %collective-permute-done.5.relayed, bf16[3,3,768,256]{3,2,1,0:T(8,128)(2,1)S(1)} %copy-done, ...), custom_call_target="tpu_custom_call" | custom-call | flops 75497472 | bytes 3866636 | tf_op jit(solution)/shard_map/pallas_call | solution.py:267
  28.6 0.6 %collective-permute-start.6 = (bf16[1,64,256]{2,1,0:T(8,128)(2,1)S(1)}, bf16[1,64,256]{2,1,0:T(8,128)(2,1)S(1)}, u32[]{:S(2)}, u32[]{:S(2)}) collective-permute-start(bf16[1,64,256]{2,1,0:T(8,128)(2,1)S(1)} %shard_map.54), channel_id=1, source_target_pairs={{0,1},{1,0},{2,3},{3,2},{4,5},{5,4},{6,7},{7,6},{8,9},{9,8},{10,11... | collective-permute-start | bytes 98312 | tf_op jit(solution)/shard_map/ppermute | solution.py:28
  29.2 1.0 %shard_map.53.total = f32[256,256]{1,0:T(8,128)S(1)} custom-call(s32[3]{0:T(128)S(1)} %shard_map.46.edges, bf16[1,4,64,256]{3,2,1,0:T(8,128)(2,1)S(1)} %collective-permute-done.3.direct, bf16[1,4,64,256]{3,2,1,0:T(8,128)(2,1)S(1)} %collective-permute-done.5.relayed, bf16[3,3,768,256]{3,2,1,0:T(8,128)(2,1)S(1)} %copy-done, f32[256,256]{1,0:T(8,128)S(1)} %get-tuple-element.17.body), custom_call_target="tpu_custom_call" | custom-call | flops 301989888 | bytes 4063244 | tf_op jit(solution)/shard_map/pallas_call | solution.py:267
  30.2 2.4 %collective-permute-done.6.above.below = bf16[1,64,256]{2,1,0:T(8,128)(2,1)S(1)} collective-permute-done((bf16[1,64,256]{2,1,0:T(8,128)(2,1)S(1)}, bf16[1,64,256]{2,1,0:T(8,128)(2,1)S(1)}, u32[]{:S(2)}, u32[]{:S(2)}) %collective-permute-start.6) | collective-permute-done | bytes 32800 | tf_op jit(solution)/shard_map/ppermute | solution.py:28
  32.6 1.3 %shard_map.55 = bf16[1,4,64,256]{3,2,1,0:T(8,128)(2,1)} custom-call(s32[3]{0:T(128)S(1)} %shard_map.46.edges, f32[256,256]{1,0:T(8,128)S(1)} %shard_map.53.total, bf16[1,64,256]{2,1,0:T(8,128)(2,1)S(1)} %collective-permute-done.6.above.below, bf16[1,64,256]{2,1,0:T(8,128)(2,1)S(1)} %collective-permute-done.6.above.below), custom_call_target="tpu_custom_call" | custom-call | flops 65536 | bytes 327692 | tf_op jit(solution)/shard_map/pallas_call | solution.py:267
Async XLA Ops:
  0.0 2.7 %copy-start.1 = (bf16[2,8,128,128]{3,2,1,0:T(8,128)(2,1)S(1)}, bf16[2,8,128,128]{3,2,1,0:T(8,128)(2,1)}, u32[]{:S(2)}) copy-start(bf16[2,8,128,128]{3,2,1,0:T(8,128)(2,1)} %frames.1) | copy-start | bytes 1572868
  0.0 8.2 %copy-start.2 = (bf16[3,3,384,128]{3,2,1,0:T(8,128)(2,1)S(1)}, bf16[3,3,384,128]{3,2,1,0:T(8,128)(2,1)}, u32[]{:S(2)}) copy-start(bf16[3,3,384,128]{3,2,1,0:T(8,128)(2,1)} %weight.9) | copy-start | bytes 2654212
  0.0 14.1 %collective-permute-start = (bf16[2,8,128,128]{3,2,1,0:T(8,128)(2,1)}, bf16[2,8,128,128]{3,2,1,0:T(8,128)(2,1)S(1)}, u32[]{:S(2)}, u32[]{:S(2)}) collective-permute-start(bf16[2,8,128,128]{3,2,1,0:T(8,128)(2,1)} %frames.1), channel_id=1, source_target_pairs={{0,2},{1,3},{2,4},{3,5},{4,6},{5,7},{6,8},{7,9},{8,10},{9,11},{10,... | collective-permute-start | bytes 1572872 | tf_op jit(solution)/shard_map/ppermute | solution.py:22
  2.7 11.4 %copy-start.3 = (bf16[3,384,256]{2,1,0:T(8,128)(2,1)S(1)}, bf16[3,384,256]{2,1,0:T(8,128)(2,1)}, u32[]{:S(2)}) copy-start(bf16[3,384,256]{2,1,0:T(8,128)(2,1)} %down.1) | copy-start | bytes 1769476
  3.3 6.5 %collective-permute-start.2 = (bf16[2,2,128,128]{3,2,1,0:T(8,128)(2,1)S(1)}, bf16[2,2,128,128]{3,2,1,0:T(8,128)(2,1)S(1)}, u32[]{:S(2)}, u32[]{:S(2)}) collective-permute-start(bf16[2,2,128,128]{3,2,1,0:T(8,128)(2,1)S(1)} %shard_map.47), channel_id=1, source_target_pairs={{0,1},{1,0},{2,3},{3,2},{4,5},{5,4},{6,7},{7,6},{8,9},{9,8},{10,11... | collective-permute-start | bytes 393224 | tf_op jit(solution)/shard_map/ppermute | solution.py:28
  4.8 9.3 %collective-permute-start.1 = (bf16[2,2,128,128]{3,2,1,0:T(8,128)(2,1)S(1)}, bf16[2,2,128,128]{3,2,1,0:T(8,128)(2,1)S(1)}, u32[]{:S(2)}, u32[]{:S(2)}) collective-permute-start(bf16[2,2,128,128]{3,2,1,0:T(8,128)(2,1)S(1)} %shard_map.47), channel_id=1, source_target_pairs={{0,3},{1,2},{2,5},{3,4},{4,7},{5,6},{6,9},{7,8},{8,11},{9,10},{10,... | collective-permute-start | bytes 393224 | tf_op jit(solution)/shard_map/ppermute | solution.py:28
  9.7 12.0 %copy-start = (bf16[3,3,768,256]{3,2,1,0:T(8,128)(2,1)S(1)}, bf16[3,3,768,256]{3,2,1,0:T(8,128)(2,1)}, u32[]{:S(2)}) copy-start(bf16[3,3,768,256]{3,2,1,0:T(8,128)(2,1)} %weight.13) | copy-start | bytes 10616836
  16.9 7.8 %collective-permute-start.4 = (bf16[1,4,64,256]{3,2,1,0:T(8,128)(2,1)S(1)}, bf16[1,4,64,256]{3,2,1,0:T(8,128)(2,1)S(1)}, u32[]{:S(2)}, u32[]{:S(2)}) collective-permute-start(bf16[1,4,64,256]{3,2,1,0:T(8,128)(2,1)S(1)} %shard_map.50.field), channel_id=1, source_target_pairs={{0,4},{1,5},{2,6},{3,7},{4,8},{5,9},{6,10},{7,11},{8,12},{9,13},{1... | collective-permute-start | bytes 393224 | tf_op jit(solution)/shard_map/ppermute | solution.py:22
  19.5 7.5 %collective-permute-start.3 = (bf16[1,4,64,256]{3,2,1,0:T(8,128)(2,1)S(1)}, bf16[1,4,64,256]{3,2,1,0:T(8,128)(2,1)S(1)}, u32[]{:S(2)}, u32[]{:S(2)}) collective-permute-start(bf16[1,4,64,256]{3,2,1,0:T(8,128)(2,1)S(1)} %shard_map.50.field), channel_id=1, source_target_pairs={{0,2},{1,3},{4,6},{5,7},{8,10},{9,11},{12,14},{13,15},{16,18},{17,... | collective-permute-start | bytes 393224 | tf_op jit(solution)/shard_map/ppermute | solution.py:35
  24.6 3.2 %collective-permute-start.5 = (bf16[1,4,64,256]{3,2,1,0:T(8,128)(2,1)S(1)}, bf16[1,4,64,256]{3,2,1,0:T(8,128)(2,1)S(1)}, u32[]{:S(2)}, u32[]{:S(2)}) collective-permute-start(bf16[1,4,64,256]{3,2,1,0:T(8,128)(2,1)S(1)} %collective-permute-done.4.field), channel_id=1, source_target_pairs={{2,0},{3,1},{6,4},{7,5},{10,8},{11,9},{14,12},{15,13},{18,16},{19,... | collective-permute-start | bytes 393224 | tf_op jit(solution)/shard_map/ppermute | solution.py:35
  28.6 4.0 %collective-permute-start.6 = (bf16[1,64,256]{2,1,0:T(8,128)(2,1)S(1)}, bf16[1,64,256]{2,1,0:T(8,128)(2,1)S(1)}, u32[]{:S(2)}, u32[]{:S(2)}) collective-permute-start(bf16[1,64,256]{2,1,0:T(8,128)(2,1)S(1)} %shard_map.54), channel_id=1, source_target_pairs={{0,1},{1,0},{2,3},{3,2},{4,5},{5,4},{6,7},{7,6},{8,9},{9,8},{10,11... | collective-permute-start | bytes 98312 | tf_op jit(solution)/shard_map/ppermute | solution.py:28

commit v4 on v3

v4 whole, which is shorter than its diff:
```python
import functools

import jax
import jax.numpy as jnp
from jax import lax
from jax.experimental import pallas as pl
from jax.experimental.pallas import tpu as pltpu
from jax.sharding import PartitionSpec as P

F32 = jnp.float32
BF16 = jnp.bfloat16


def moved(value, steps, hop):
    tm, rows = lax.axis_size("tm"), lax.axis_size("rows")
    pairs = [
        (t * rows + r, (t + steps) * rows + r + hop)
        for t in range(tm - steps)
        for r in range(rows)
        if 0 <= r + hop < rows
    ]
    return lax.ppermute(value, ("tm", "rows"), pairs)


def ring(value, steps):
    tm = lax.axis_size("tm")
    return lax.ppermute(value, "tm", [(t, (t + steps) % tm) for t in range(tm)])


def swapped(value, steps):
    tm = lax.axis_size("tm")
    pairs = [(t * 2 + r, (t + steps) * 2 + 1 - r) for t in range(tm - steps) for r in range(2)]
    return lax.ppermute(value, ("tm", "rows"), pairs)


def paired(value):
    return lax.ppermute(value, "tm", [(t, t ^ 1) for t in range(lax.axis_size("tm"))])


def has_above():
    return lax.axis_index("rows") > 0


def has_below():
    return lax.axis_index("rows") < lax.axis_size("rows") - 1


def has_earlier(steps):
    return lax.axis_index("tm") >= steps


def pace_kernel(out):
    out[...] = jnp.zeros_like(out)


def edge_kernel(_, cells, out):
    width = out.shape[1]
    first = (1 - lax.axis_index("rows")) * (cells.shape[1] - width)
    out[...] = cells[:, pl.ds(first, width)]


def frame_rims(pace, frames):
    rows = frames.shape[1]
    if lax.axis_size("rows") == 2:
        sent = call(
            edge_kernel,
            jax.ShapeDtypeStruct((frames.shape[0], 2, *frames.shape[2:]), BF16),
            [],
            0,
            (pace, frames),
        )
        return [(both, both) for both in (swapped(sent, 0), swapped(sent, 1))]
    head, tail = frames[:, :2], frames[:, rows - 1 :]
    return [(moved(tail, steps, 1), moved(head, steps, -1)) for steps in (0, 1)]


def column_shift(value, cols, steps):
    size = value.shape[0]
    column = lax.broadcasted_iota(jnp.int32, value.shape, 0) % cols
    edge = 0 if steps > 0 else cols - 1
    return jnp.where(column == edge, 0.0, pltpu.roll(value, steps % size, 0))


def shifted_columns(flat, cols):
    wide = flat.astype(F32)
    return column_shift(wide, cols, 1).astype(BF16), column_shift(wide, cols, -1).astype(BF16)


def tap_matrix(weight, first_tap, row_taps, e, channels):
    zero = jnp.zeros((channels, channels), BF16)

    def pick(tap, b):
        return weight[tap, b, e * channels : (e + 1) * channels] if 0 <= tap <= 2 else zero

    return jnp.concatenate(
        [
            jnp.concatenate([pick(first_tap + f, b), pick(first_tap + f - 1, b)], axis=1)
            for f in range(2)
            for b in row_taps
        ],
        axis=0,
    )


def fine_rows(row, outs, row_taps, weight, first_tap):
    channels = weight.shape[-1]
    some = next(x for f in range(2) for r in outs for b in row_taps if (x := row(f, r - 1 + b)) is not None)
    cols = some.shape[0]
    zero = jnp.zeros((cols, channels), BF16)

    def cell(f, i):
        found = row(f, i)
        return zero if found is None else found

    left = jnp.concatenate(
        [
            jnp.concatenate([cell(f, r - 1 + b) for f in range(2) for b in row_taps], axis=1)
            for r in outs
        ],
        axis=0,
    )
    sums = [
        jnp.dot(
            left, tap_matrix(weight, first_tap, row_taps, e, channels), preferred_element_type=F32
        )
        for e in range(3)
    ]
    return sums[1] + column_shift(sums[0], cols, 1) + column_shift(sums[2], cols, -1)


def chunks_of(count):
    size = next(c for c in (3, 2, 1) if count % c == 0)
    return [range(i, i + size) for i in range(0, count, size)]


def fine_own_kernel(frames, weight, out):
    _, rows, cols, _ = frames.shape

    def row(f, i):
        return frames[f, i] if 0 <= i < rows else None

    for outs in chunks_of(rows + 1):
        out[outs[0] * cols : (outs[-1] + 1) * cols] = fine_rows(row, outs, range(3), weight, 2)


def halo_row(above, below, rows):
    def row(f, i):
        if i == -1:
            cells, have = above[f, above.shape[1] - 1], has_above()
        elif i >= rows:
            cells, have = below[f, i - rows], has_below()
        else:
            return None
        return jnp.where(have, cells, jnp.zeros_like(cells))

    return row


def fine_halo_kernel(above, below, weight, out, *, rows):
    cols = above.shape[2]
    row = halo_row(above, below, rows)
    out[:cols] = fine_rows(row, [0], [0], weight, 2)
    out[cols:] = fine_rows(row, [rows - 1, rows], [1, 2], weight, 2)


def silu(v):
    return v / (1.0 + jnp.exp(-v))


def fine_rest_kernel(frames, above, below, weight, own, halo, down, out, pooled):
    _, rows, cols, channels = frames.shape
    outside = halo_row(above, below, rows)

    def row(f, i):
        return frames[f, i] if 0 <= i < rows else outside(f, i)

    pad = pooled.shape[1] - cols
    pooled[:, cols:] = jnp.zeros((rows + 1, pad, channels), F32)
    for outs in chunks_of(rows + 1):
        total = fine_rows(row, outs, range(3), weight, 0)
        for i, r in enumerate(outs):
            line = jnp.where(has_earlier(1), total[i * cols : (i + 1) * cols], 0.0)
            line = line + own[r * cols : (r + 1) * cols]
            for k, halo_r in enumerate((0, rows - 1, rows)):
                if r == halo_r:
                    line = line + halo[k * cols : (k + 1) * cols]
            fine = silu(line).astype(BF16).astype(F32)
            mean = ((fine[:, :channels] + fine[:, channels:]) * 0.5).astype(BF16).astype(F32)
            if r == rows:
                mean = jnp.where(has_below(), mean, 0.0)
            pooled[r, :cols] = mean
    strips = []
    for p in range(rows // 2):
        pieces = [
            pooled[2 * p + b, pl.ds(e, cols // 2, stride=2), :].astype(BF16)
            for b in range(3)
            for e in range(3)
        ]
        strips.append(jnp.concatenate(pieces, axis=1))
    left = jnp.concatenate(strips, axis=0)
    right = down[...].reshape(-1, down.shape[-1])
    out[...] = jnp.dot(left, right, preferred_element_type=F32).astype(BF16).reshape(out.shape)


def field_taps(field):
    _, rows, cols, channels = field.shape
    flat = field.reshape(rows * cols, channels)
    left, right = shifted_columns(flat, cols)
    return jnp.concatenate([left, flat, right], axis=1)


def rim_sum(taps, weight, a, cols, both):
    size = taps.shape[0]
    dot = functools.partial(jnp.dot, preferred_element_type=F32)
    if both:
        return [dot(taps[:cols], weight[a, 2]), dot(taps[size - cols :], weight[a, 0])]
    row = jnp.where(has_above(), taps[:cols], taps[size - cols :])
    return [dot(row, weight[a, 2 * lax.axis_index("rows")])]


def body_sum(taps, weight, a, cols):
    size = taps.shape[0]
    dot = functools.partial(jnp.dot, preferred_element_type=F32)
    zero = jnp.zeros((cols, weight.shape[-1]), F32)
    upper = jnp.concatenate([zero, dot(taps[: size - cols], weight[a, 0])], axis=0)
    lower = jnp.concatenate([dot(taps[cols:], weight[a, 2]), zero], axis=0)
    return dot(taps, weight[a, 1]) + upper + lower


def coarse_first_kernel(field, weight, body, rim):
    taps = field_taps(field[...])
    cols = field.shape[2]
    body[...] = body_sum(taps, weight, 2, cols)
    for i, part in enumerate(rim_sum(taps, weight, 2, cols, rim.shape[0] == 2)):
        rim[i] = part


def coarse_next_kernel(field, weight, body_in, rim_in, body, rim):
    cells = field[...]
    taps = field_taps(jnp.where(has_earlier(2), cells, jnp.zeros_like(cells)))
    cols = field.shape[2]
    body[...] = body_in[...] + body_sum(taps, weight, 0, cols)
    for i, part in enumerate(rim_sum(taps, weight, 0, cols, rim.shape[0] == 2)):
        rim[i] = rim_in[i] + part


def middle_taps(direct, relayed):
    cells = jnp.where(lax.axis_index("tm") % 2 == 1, direct[...], relayed[...])
    return field_taps(jnp.where(has_earlier(1), cells, jnp.zeros_like(cells)))


def coarse_rim_kernel(direct, relayed, weight, rim, out):
    cols = direct.shape[2]
    taps = middle_taps(direct, relayed)
    for i, part in enumerate(rim_sum(taps, weight, 1, cols, rim.shape[0] == 2)):
        out[i] = (rim[i] + part).astype(BF16)


def coarse_last_kernel(direct, relayed, weight, body, out):
    cols = direct.shape[2]
    taps = middle_taps(direct, relayed)
    out[...] = body[...] + body_sum(taps, weight, 1, cols)


def finish_kernel(total, above, below, out):
    _, rows, cols, channels = out.shape
    for p in range(rows):
        row = total[p * cols : (p + 1) * cols]
        if p == 0:
            row = row + jnp.where(has_above(), above[0].astype(F32), 0.0)
        if p == rows - 1:
            row = row + jnp.where(has_below(), below[0].astype(F32), 0.0)
        out[0, p] = silu(row).astype(BF16)


def call(kernel, out_shape, scratch, flops, args):
    size = sum(a.size * a.dtype.itemsize for a in args)
    return pl.pallas_call(
        kernel,
        out_shape=out_shape,
        in_specs=[pl.BlockSpec(memory_space=pltpu.VMEM)] * len(args),
        out_specs=jax.tree.map(lambda _: pl.BlockSpec(memory_space=pltpu.VMEM), out_shape),
        scratch_shapes=scratch,
        cost_estimate=pl.CostEstimate(flops=flops, bytes_accessed=size, transcendentals=0),
        compiler_params=pltpu.CompilerParams(vmem_limit_bytes=20 * 1024 * 1024),
    )(*args)


def local(frames, conv_fine, conv_down, conv_coarse):
    _, rows, cols, channels = frames.shape
    wide = conv_down.shape[-1]
    strips, times = lax.axis_size("rows"), lax.axis_size("tm")
    pace = call(pace_kernel, jax.ShapeDtypeStruct((8, 128), F32), [], 4 * 10**9, ())

    earlier = ring(frames, 1)
    (above, below), (above_1, below_1) = frame_rims(pace, frames)
    size = (rows + 1) * cols
    pair = jax.ShapeDtypeStruct((size, 2 * channels), F32)
    flops = 2 * size * 18 * channels * 2 * channels
    own = call(fine_own_kernel, pair, [], flops, (frames, conv_fine))
    halo = call(
        functools.partial(fine_halo_kernel, rows=rows),
        jax.ShapeDtypeStruct((3 * cols, 2 * channels), F32),
        [],
        flops // 3,
        (above, below, conv_fine),
    )
    half_rows, half_cols = rows // 2, cols // 2
    shape = jax.ShapeDtypeStruct((1, half_rows, half_cols, wide), BF16)
    field = call(
        fine_rest_kernel,
        shape,
        [pltpu.VMEM((rows + 1, cols + 8, channels), F32)],
        flops,
        (earlier, above_1, below_1, conv_fine, own, halo, conv_down),
    )
    sides = 1 if strips == 2 else 2
    sums = jax.ShapeDtypeStruct((half_rows * half_cols, wide), F32)
    rims = jax.ShapeDtypeStruct((sides, half_cols, wide), F32)
    flops = 2 * half_rows * half_cols * 9 * wide * wide
    field_2 = ring(field, 2)
    body, rim = call(coarse_first_kernel, (sums, rims), [], flops, (field, conv_coarse))
    field_2, body, rim = lax.optimization_barrier((field_2, body, rim))
    if times % 2 == 0:
        direct, relayed = paired(field), paired(field_2)
    else:
        direct = relayed = moved(field, 1, 0)
    body, rim = call(
        coarse_next_kernel, (sums, rims), [], flops, (field_2, conv_coarse, body, rim)
    )
    rim = call(
        coarse_rim_kernel,
        jax.ShapeDtypeStruct(rims.shape, BF16),
        [],
        flops // 4,
        (direct, relayed, conv_coarse, rim),
    )
    if sides == 1:
        from_above = from_below = swapped(rim, 0)
    else:
        from_above, from_below = moved(rim[1:], 0, 1), moved(rim[:1], 0, -1)
    total = call(coarse_last_kernel, sums, [], flops, (direct, relayed, conv_coarse, body))
    return call(finish_kernel, shape, [], sums.size, (total, from_above, from_below))


def solution(mesh):
    placed = (P("tm", "rows", None, None), P(), P(), P())
    return jax.shard_map(
        local, mesh=mesh, in_specs=placed, out_specs=P("tm", "rows", None, None), check_vma=False
    )
```

time: 34.1 us -> 29 us (0.85)
  the two profiles are of different devices: /device:TPU:16 before, /device:TPU:0 now
where the time goes in v4:
time: 29 us; the launch traced here: 28.8 us
  waiting for transfers between devices  12.2 us (42%)
  starting transfers between devices  9.46 us (33%)
  Pallas kernels  6.56 us (23%)
  local copies, waits for them, and re-layouts  0.56 us (2%)
    ppermute x2, waiting for transfers between devices, ring(): return lax.ppermute(value, 'tm', [(t, (t + steps) % tm) for t in range(tm)])  9.19 us
    ppermute x3, starting transfers between devices, swapped(): return lax.ppermute(value, ('tm', 'rows'), pairs)  7.36 us
    pallas_call x10, Pallas kernels, call(): pl.pallas_call(kernel, out_shape=out_shape, in_specs=[pl.BlockSpec(memory...  6.56 us
    ppermute x3, waiting for transfers between devices, swapped(): return lax.ppermute(value, ('tm', 'rows'), pairs)  2.13 us
    ppermute x2, starting transfers between devices, ring(): return lax.ppermute(value, 'tm', [(t, (t + steps) % tm) for t in range(tm)])  2.1 us
    ppermute x2, waiting for transfers between devices, paired(): lax.ppermute(value, 'tm', [(t, t ^ 1) for t in range(lax.axis_size('tm'))])  0.85 us
  transfers between devices with their start and end apart: 7, of which 6 were waited for; matrix products, arithmetic and copies ran while one was open for 0% of the time, Pallas kernels for 12%

profile of v4, /device:TPU:0, one launch (start us, length us, event | category | flops | bytes accessed | tf_op | source)
XLA Modules:
  0.0 28.8 jit_solution(5941231626595852465)
XLA Ops:
  0.0 0.0 copy-start.1
  0.0 0.0 copy-start.2
  0.0 0.5 %collective-permute-start = (bf16[2,8,128,128]{3,2,1,0:T(8,128)(2,1)}, bf16[2,8,128,128]{3,2,1,0:T(8,128)(2,1)S(1)}, u32[]{:S(2)}, u32[]{:S(2)}) collective-permute-start(bf16[2,8,128,128]{3,2,1,0:T(8,128)(2,1)} %frames.1), channel_id=1, source_target_pairs={{0,2},{2,4},{4,6},{6,8},{8,10},{10,12},{12,14},{14,16},{16,18},{18... | collective-permute-start | bytes 1572872 | tf_op jit(solution)/shard_map/ppermute | solution.py:27
  0.5 0.5 %copy-done.1 = bf16[2,8,128,128]{3,2,1,0:T(8,128)(2,1)S(1)} copy-done((bf16[2,8,128,128]{3,2,1,0:T(8,128)(2,1)S(1)}, bf16[2,8,128,128]{3,2,1,0:T(8,128)(2,1)}, u32[]{:S(2)}) %copy-start.1) | copy-done | bytes 524312
  1.0 0.0 copy-start.3
  1.1 3.1 %collective-permute-start.2 = (bf16[2,2,128,128]{3,2,1,0:T(8,128)(2,1)S(1)}, bf16[2,2,128,128]{3,2,1,0:T(8,128)(2,1)S(1)}, u32[]{:S(2)}, u32[]{:S(2)}) collective-permute-start(bf16[2,2,128,128]{3,2,1,0:T(8,128)(2,1)S(1)} %shard_map.47), channel_id=1, source_target_pairs={{0,1},{1,0},{2,3},{3,2},{4,5},{5,4},{6,7},{7,6},{8,9},{9,8},{10,11... | collective-permute-start | bytes 393224 | tf_op jit(solution)/shard_map/ppermute | solution.py:33
  4.1 2.3 %collective-permute-start.1 = (bf16[2,2,128,128]{3,2,1,0:T(8,128)(2,1)S(1)}, bf16[2,2,128,128]{3,2,1,0:T(8,128)(2,1)S(1)}, u32[]{:S(2)}, u32[]{:S(2)}) collective-permute-start(bf16[2,2,128,128]{3,2,1,0:T(8,128)(2,1)S(1)} %shard_map.47), channel_id=1, source_target_pairs={{0,3},{1,2},{2,5},{3,4},{4,7},{5,6},{6,9},{7,8},{8,11},{9,10},{10,... | collective-permute-start | bytes 393224 | tf_op jit(solution)/shard_map/ppermute | solution.py:33
  6.4 0.0 copy-done.2
  6.4 1.5 %shard_map.48.own = f32[1152,256]{1,0:T(8,128)S(1)} custom-call(bf16[2,8,128,128]{3,2,1,0:T(8,128)(2,1)S(1)} %copy-done.1, bf16[3,3,384,128]{3,2,1,0:T(8,128)(2,1)S(1)} %copy-done.2), custom_call_target="tpu_custom_call" | custom-call | flops 1358954496 | bytes 1409024 | tf_op jit(solution)/shard_map/pallas_call | solution.py:278
  8.0 0.0 copy-start
  8.0 0.4 %collective-permute-done.2.above.below = bf16[2,2,128,128]{3,2,1,0:T(8,128)(2,1)S(1)} collective-permute-done((bf16[2,2,128,128]{3,2,1,0:T(8,128)(2,1)S(1)}, bf16[2,2,128,128]{3,2,1,0:T(8,128)(2,1)S(1)}, u32[]{:S(2)}, u32[]{:S(2)}) %collective-permute-start.2) | collective-permute-done | bytes 131104 | tf_op jit(solution)/shard_map/ppermute | solution.py:33
  8.4 0.4 %shard_map.49.halo = f32[384,256]{1,0:T(8,128)S(1)} custom-call(bf16[2,2,128,128]{3,2,1,0:T(8,128)(2,1)S(1)} %collective-permute-done.2.above.below, bf16[2,2,128,128]{3,2,1,0:T(8,128)(2,1)S(1)} %collective-permute-done.2.above.below, bf16[3,3,384,128]{3,2,1,0:T(8,128)(2,1)S(1)} %copy-done.2), custom_call_target="tpu_custom_call" | custom-call | flops 452984832 | bytes 1146880 | tf_op jit(solution)/shard_map/pallas_call | solution.py:278
  8.8 0.2 collective-permute-done.1.above.below
  9.0 3.6 %collective-permute-done.frames = bf16[2,8,128,128]{3,2,1,0:T(8,128)(2,1)S(1)} collective-permute-done((bf16[2,8,128,128]{3,2,1,0:T(8,128)(2,1)}, bf16[2,8,128,128]{3,2,1,0:T(8,128)(2,1)S(1)}, u32[]{:S(2)}, u32[]{:S(2)}) %collective-permute-start) | collective-permute-done | bytes 524320 | tf_op jit(solution)/shard_map/ppermute | solution.py:27
  12.6 0.0 copy-done.3
  12.6 2.2 %shard_map.50.field = bf16[1,4,64,256]{3,2,1,0:T(8,128)(2,1)S(1)} custom-call(bf16[2,8,128,128]{3,2,1,0:T(8,128)(2,1)S(1)} %collective-permute-done.frames, bf16[2,2,128,128]{3,2,1,0:T(8,128)(2,1)S(1)} %collective-permute-done.1.above.below, bf16[2,2,128,128]{3,2,1,0:T(8,128)(2,1)S(1)} %collective-permute-done.1.above.below, ...), custom_call_target="tpu_custom_call" | custom-call | flops 1358954496 | bytes 3833856 | tf_op jit(solution)/shard_map/pallas_call | solution.py:278
  14.8 1.6 %collective-permute-start.4 = (bf16[1,4,64,256]{3,2,1,0:T(8,128)(2,1)S(1)}, bf16[1,4,64,256]{3,2,1,0:T(8,128)(2,1)S(1)}, u32[]{:S(2)}, u32[]{:S(2)}) collective-permute-start(bf16[1,4,64,256]{3,2,1,0:T(8,128)(2,1)S(1)} %shard_map.50.field), channel_id=1, source_target_pairs={{0,4},{2,6},{4,8},{6,10},{8,12},{10,14},{12,16},{14,18},{16,20},{1... | collective-permute-start | bytes 393224 | tf_op jit(solution)/shard_map/ppermute | solution.py:27
  16.5 0.0 collective-permute-start.3
  16.5 0.0 copy-done
  16.5 0.5 %shard_map.51 = (f32[256,256]{1,0:T(8,128)S(1)}, f32[1,64,256]{2,1,0:T(8,128)S(1)}) custom-call(bf16[1,4,64,256]{3,2,1,0:T(8,128)(2,1)S(1)} %shard_map.50.field, bf16[3,3,768,256]{3,2,1,0:T(8,128)(2,1)S(1)} %copy-done), custom_call_target="tpu_custom_call" | custom-call | flops 301989888 | bytes 3670016 | tf_op jit(solution)/shard_map/pallas_call | solution.py:278
  17.0 5.6 %collective-permute-done.4.field = bf16[1,4,64,256]{3,2,1,0:T(8,128)(2,1)S(1)} collective-permute-done((bf16[1,4,64,256]{3,2,1,0:T(8,128)(2,1)S(1)}, bf16[1,4,64,256]{3,2,1,0:T(8,128)(2,1)S(1)}, u32[]{:S(2)}, u32[]{:S(2)}) %collective-permute-start.4) | collective-permute-done | bytes 131104 | tf_op jit(solution)/shard_map/ppermute | solution.py:27
  22.6 0.0 collective-permute-start.5
  22.6 0.5 %shard_map.52 = (f32[256,256]{1,0:T(8,128)S(1)}, f32[1,64,256]{2,1,0:T(8,128)S(1)}) custom-call(bf16[1,4,64,256]{3,2,1,0:T(8,128)(2,1)S(1)} %collective-permute-done.4.field, bf16[3,3,768,256]{3,2,1,0:T(8,128)(2,1)S(1)} %copy-done, f32[256,256]{1,0:T(8,128)S(1)} %get-tuple-element.15.body_in, f32[1,64,256]{2,1,0:T(8,128)S(1)} %get-tuple-element.16.rim_in), custom_call_target="tpu_custom_call" | custom-call | flops 301989888 | bytes 3997696 | tf_op jit(solution)/shard_map/pallas_call | solution.py:278
  23.1 0.0 collective-permute-done.3.direct
  23.1 0.8 %collective-permute-done.5.relayed = bf16[1,4,64,256]{3,2,1,0:T(8,128)(2,1)S(1)} collective-permute-done((bf16[1,4,64,256]{3,2,1,0:T(8,128)(2,1)S(1)}, bf16[1,4,64,256]{3,2,1,0:T(8,128)(2,1)S(1)}, u32[]{:S(2)}, u32[]{:S(2)}) %collective-permute-start.5) | collective-permute-done | bytes 131104 | tf_op jit(solution)/shard_map/ppermute | solution.py:37
  23.9 0.2 shard_map.54
  24.1 2.0 %collective-permute-start.6 = (bf16[1,64,256]{2,1,0:T(8,128)(2,1)S(1)}, bf16[1,64,256]{2,1,0:T(8,128)(2,1)S(1)}, u32[]{:S(2)}, u32[]{:S(2)}) collective-permute-start(bf16[1,64,256]{2,1,0:T(8,128)(2,1)S(1)} %shard_map.54), channel_id=1, source_target_pairs={{0,1},{1,0},{2,3},{3,2},{4,5},{5,4},{6,7},{7,6},{8,9},{9,8},{10,11... | collective-permute-start | bytes 98312 | tf_op jit(solution)/shard_map/ppermute | solution.py:33
  26.1 0.4 %shard_map.53.total = f32[256,256]{1,0:T(8,128)S(1)} custom-call(bf16[1,4,64,256]{3,2,1,0:T(8,128)(2,1)S(1)} %collective-permute-done.3.direct, bf16[1,4,64,256]{3,2,1,0:T(8,128)(2,1)S(1)} %collective-permute-done.5.relayed, bf16[3,3,768,256]{3,2,1,0:T(8,128)(2,1)S(1)} %copy-done, f32[256,256]{1,0:T(8,128)S(1)} %get-tuple-element.17.body), custom_call_target="tpu_custom_call" | custom-call | flops 301989888 | bytes 4063232 | tf_op jit(solution)/shard_map/pallas_call | solution.py:278
  26.5 1.6 %collective-permute-done.6.above.below = bf16[1,64,256]{2,1,0:T(8,128)(2,1)S(1)} collective-permute-done((bf16[1,64,256]{2,1,0:T(8,128)(2,1)S(1)}, bf16[1,64,256]{2,1,0:T(8,128)(2,1)S(1)}, u32[]{:S(2)}, u32[]{:S(2)}) %collective-permute-start.6) | collective-permute-done | bytes 32800 | tf_op jit(solution)/shard_map/ppermute | solution.py:33
  28.1 0.7 %shard_map.55 = bf16[1,4,64,256]{3,2,1,0:T(8,128)(2,1)} custom-call(f32[256,256]{1,0:T(8,128)S(1)} %shard_map.53.total, bf16[1,64,256]{2,1,0:T(8,128)(2,1)S(1)} %collective-permute-done.6.above.below, bf16[1,64,256]{2,1,0:T(8,128)(2,1)S(1)} %collective-permute-done.6.above.below), custom_call_target="tpu_custom_call" | custom-call | flops 65536 | bytes 327680 | tf_op jit(solution)/shard_map/pallas_call | solution.py:278
  (2 shorter events, 0.0 us)
Async XLA Ops:
  0.0 1.0 %copy-start.1 = (bf16[2,8,128,128]{3,2,1,0:T(8,128)(2,1)S(1)}, bf16[2,8,128,128]{3,2,1,0:T(8,128)(2,1)}, u32[]{:S(2)}) copy-start(bf16[2,8,128,128]{3,2,1,0:T(8,128)(2,1)} %frames.1) | copy-start | bytes 1572868
  0.0 6.4 %copy-start.2 = (bf16[3,3,384,128]{3,2,1,0:T(8,128)(2,1)S(1)}, bf16[3,3,384,128]{3,2,1,0:T(8,128)(2,1)}, u32[]{:S(2)}) copy-start(bf16[3,3,384,128]{3,2,1,0:T(8,128)(2,1)} %weight.9) | copy-start | bytes 2654212
  0.0 12.6 %collective-permute-start = (bf16[2,8,128,128]{3,2,1,0:T(8,128)(2,1)}, bf16[2,8,128,128]{3,2,1,0:T(8,128)(2,1)S(1)}, u32[]{:S(2)}, u32[]{:S(2)}) collective-permute-start(bf16[2,8,128,128]{3,2,1,0:T(8,128)(2,1)} %frames.1), channel_id=1, source_target_pairs={{0,2},{2,4},{4,6},{6,8},{8,10},{10,12},{12,14},{14,16},{16,18},{18... | collective-permute-start | bytes 1572872 | tf_op jit(solution)/shard_map/ppermute | solution.py:27
  1.0 11.6 %copy-start.3 = (bf16[3,384,256]{2,1,0:T(8,128)(2,1)S(1)}, bf16[3,384,256]{2,1,0:T(8,128)(2,1)}, u32[]{:S(2)}) copy-start(bf16[3,384,256]{2,1,0:T(8,128)(2,1)} %down.1) | copy-start | bytes 1769476
  1.1 7.3 %collective-permute-start.2 = (bf16[2,2,128,128]{3,2,1,0:T(8,128)(2,1)S(1)}, bf16[2,2,128,128]{3,2,1,0:T(8,128)(2,1)S(1)}, u32[]{:S(2)}, u32[]{:S(2)}) collective-permute-start(bf16[2,2,128,128]{3,2,1,0:T(8,128)(2,1)S(1)} %shard_map.47), channel_id=1, source_target_pairs={{0,1},{1,0},{2,3},{3,2},{4,5},{5,4},{6,7},{7,6},{8,9},{9,8},{10,11... | collective-permute-start | bytes 393224 | tf_op jit(solution)/shard_map/ppermute | solution.py:33
  4.1 4.9 %collective-permute-start.1 = (bf16[2,2,128,128]{3,2,1,0:T(8,128)(2,1)S(1)}, bf16[2,2,128,128]{3,2,1,0:T(8,128)(2,1)S(1)}, u32[]{:S(2)}, u32[]{:S(2)}) collective-permute-start(bf16[2,2,128,128]{3,2,1,0:T(8,128)(2,1)S(1)} %shard_map.47), channel_id=1, source_target_pairs={{0,3},{1,2},{2,5},{3,4},{4,7},{5,6},{6,9},{7,8},{8,11},{9,10},{10,... | collective-permute-start | bytes 393224 | tf_op jit(solution)/shard_map/ppermute | solution.py:33
  8.0 8.5 %copy-start = (bf16[3,3,768,256]{3,2,1,0:T(8,128)(2,1)S(1)}, bf16[3,3,768,256]{3,2,1,0:T(8,128)(2,1)}, u32[]{:S(2)}) copy-start(bf16[3,3,768,256]{3,2,1,0:T(8,128)(2,1)} %weight.13) | copy-start | bytes 10616836
  14.8 7.7 %collective-permute-start.4 = (bf16[1,4,64,256]{3,2,1,0:T(8,128)(2,1)S(1)}, bf16[1,4,64,256]{3,2,1,0:T(8,128)(2,1)S(1)}, u32[]{:S(2)}, u32[]{:S(2)}) collective-permute-start(bf16[1,4,64,256]{3,2,1,0:T(8,128)(2,1)S(1)} %shard_map.50.field), channel_id=1, source_target_pairs={{0,4},{2,6},{4,8},{6,10},{8,12},{10,14},{12,16},{14,18},{16,20},{1... | collective-permute-start | bytes 393224 | tf_op jit(solution)/shard_map/ppermute | solution.py:27
  16.5 6.6 %collective-permute-start.3 = (bf16[1,4,64,256]{3,2,1,0:T(8,128)(2,1)S(1)}, bf16[1,4,64,256]{3,2,1,0:T(8,128)(2,1)S(1)}, u32[]{:S(2)}, u32[]{:S(2)}) collective-permute-start(bf16[1,4,64,256]{3,2,1,0:T(8,128)(2,1)S(1)} %shard_map.50.field), channel_id=1, source_target_pairs={{0,2},{2,0},{4,6},{6,4},{8,10},{10,8},{12,14},{14,12},{16,18},{18,... | collective-permute-start | bytes 393224 | tf_op jit(solution)/shard_map/ppermute | solution.py:37
  22.6 1.3 %collective-permute-start.5 = (bf16[1,4,64,256]{3,2,1,0:T(8,128)(2,1)S(1)}, bf16[1,4,64,256]{3,2,1,0:T(8,128)(2,1)S(1)}, u32[]{:S(2)}, u32[]{:S(2)}) collective-permute-start(bf16[1,4,64,256]{3,2,1,0:T(8,128)(2,1)S(1)} %collective-permute-done.4.field), channel_id=1, source_target_pairs={{0,2},{2,0},{4,6},{6,4},{8,10},{10,8},{12,14},{14,12},{16,18},{18,... | collective-permute-start | bytes 393224 | tf_op jit(solution)/shard_map/ppermute | solution.py:37
  24.1 4.0 %collective-permute-start.6 = (bf16[1,64,256]{2,1,0:T(8,128)(2,1)S(1)}, bf16[1,64,256]{2,1,0:T(8,128)(2,1)S(1)}, u32[]{:S(2)}, u32[]{:S(2)}) collective-permute-start(bf16[1,64,256]{2,1,0:T(8,128)(2,1)S(1)} %shard_map.54), channel_id=1, source_target_pairs={{0,1},{1,0},{2,3},{3,2},{4,5},{5,4},{6,7},{7,6},{8,9},{9,8},{10,11... | collective-permute-start | bytes 98312 | tf_op jit(solution)/shard_map/ppermute | solution.py:33

commit v5 on v4

--- a/solution.py
+++ b/solution.py
@@ -167,7 +167,7 @@
     return v / (1.0 + jnp.exp(-v))
 
 
-def fine_rest_kernel(frames, above, below, weight, own, halo, down, out, pooled):
+def fine_rest_kernel(frames, above, below, weight, own, halo, down, out, rim, pooled):
     _, rows, cols, channels = frames.shape
     outside = halo_row(above, below, rows)
 
@@ -199,78 +199,53 @@
         strips.append(jnp.concatenate(pieces, axis=1))
     left = jnp.concatenate(strips, axis=0)
     right = down[...].reshape(-1, down.shape[-1])
-    out[...] = jnp.dot(left, right, preferred_element_type=F32).astype(BF16).reshape(out.shape)
-
-
-def field_taps(field):
+    reduced = jnp.dot(left, right, preferred_element_type=F32).astype(BF16)
+    out[...] = reduced.reshape(out.shape)
+    head, tail = reduced[: cols // 2], reduced[reduced.shape[0] - cols // 2 :]
+    if rim.shape[0] == 1:
+        rim[0] = jnp.where(has_above(), head, tail)
+    else:
+        rim[0], rim[1] = head, tail
+
+
+def coarse_sum(field, rim, weight, a):
     _, rows, cols, channels = field.shape
-    flat = field.reshape(rows * cols, channels)
+    zero = jnp.zeros((cols, channels), BF16)
+    flat = jnp.concatenate(
+        [
+            jnp.where(has_above(), rim[0], zero),
+            field.reshape(rows * cols, channels),
+            jnp.where(has_below(), rim[rim.shape[0] - 1], zero),
+        ],
+        axis=0,
+    )
     left, right = shifted_columns(flat, cols)
-    return jnp.concatenate([left, flat, right], axis=1)
-
-
-def rim_sum(taps, weight, a, cols, both):
-    size = taps.shape[0]
-    dot = functools.partial(jnp.dot, preferred_element_type=F32)
-    if both:
-        return [dot(taps[:cols], weight[a, 2]), dot(taps[size - cols :], weight[a, 0])]
-    row = jnp.where(has_above(), taps[:cols], taps[size - cols :])
-    return [dot(row, weight[a, 2 * lax.axis_index("rows")])]
-
-
-def body_sum(taps, weight, a, cols):
-    size = taps.shape[0]
-    dot = functools.partial(jnp.dot, preferred_element_type=F32)
-    zero = jnp.zeros((cols, weight.shape[-1]), F32)
-    upper = jnp.concatenate([zero, dot(taps[: size - cols], weight[a, 0])], axis=0)
-    lower = jnp.concatenate([dot(taps[cols:], weight[a, 2]), zero], axis=0)
-    return dot(taps, weight[a, 1]) + upper + lower
-
-
-def coarse_first_kernel(field, weight, body, rim):
-    taps = field_taps(field[...])
-    cols = field.shape[2]
-    body[...] = body_sum(taps, weight, 2, cols)
-    for i, part in enumerate(rim_sum(taps, weight, 2, cols, rim.shape[0] == 2)):
-        rim[i] = part
-
-
-def coarse_next_kernel(field, weight, body_in, rim_in, body, rim):
-    cells = field[...]
-    taps = field_taps(jnp.where(has_earlier(2), cells, jnp.zeros_like(cells)))
-    cols = field.shape[2]
-    body[...] = body_in[...] + body_sum(taps, weight, 0, cols)
-    for i, part in enumerate(rim_sum(taps, weight, 0, cols, rim.shape[0] == 2)):
-        rim[i] = rim_in[i] + part
-
-
-def middle_taps(direct, relayed):
-    cells = jnp.where(lax.axis_index("tm") % 2 == 1, direct[...], relayed[...])
-    return field_taps(jnp.where(has_earlier(1), cells, jnp.zeros_like(cells)))
-
-
-def coarse_rim_kernel(direct, relayed, weight, rim, out):
-    cols = direct.shape[2]
-    taps = middle_taps(direct, relayed)
-    for i, part in enumerate(rim_sum(taps, weight, 1, cols, rim.shape[0] == 2)):
-        out[i] = (rim[i] + part).astype(BF16)
-
-
-def coarse_last_kernel(direct, relayed, weight, body, out):
-    cols = direct.shape[2]
-    taps = middle_taps(direct, relayed)
-    out[...] = body[...] + body_sum(taps, weight, 1, cols)
-
-
-def finish_kernel(total, above, below, out):
-    _, rows, cols, channels = out.shape
-    for p in range(rows):
-        row = total[p * cols : (p + 1) * cols]
-        if p == 0:
-            row = row + jnp.where(has_above(), above[0].astype(F32), 0.0)
-        if p == rows - 1:
-            row = row + jnp.where(has_below(), below[0].astype(F32), 0.0)
-        out[0, p] = silu(row).astype(BF16)
+    taps = jnp.concatenate([left, flat, right], axis=1)
+    total = None
+    for b in range(3):
+        part = jnp.dot(
+            taps[b * cols : (b + rows) * cols], weight[a, b], preferred_element_type=F32
+        )
+        total = part if total is None else total + part
+    return total
+
+
+def coarse_first_kernel(field, rim, weight, out):
+    out[...] = coarse_sum(field[...], rim[...], weight, 2)
+
+
+def coarse_next_kernel(field, rim, weight, total, out):
+    part = coarse_sum(field[...], rim[...], weight, 0)
+    out[...] = total[...] + jnp.where(has_earlier(2), part, 0.0)
+
+
+def coarse_last_kernel(direct, direct_rim, relayed, relayed_rim, weight, total, out):
+    odd = lax.axis_index("tm") % 2 == 1
+    field = jnp.where(odd, direct[...], relayed[...])
+    rim = jnp.where(odd, direct_rim[...], relayed_rim[...])
+    part = coarse_sum(field, rim, weight, 1)
+    total = total[...] + jnp.where(has_earlier(1), part, 0.0)
+    out[...] = silu(total).astype(BF16).reshape(out.shape)
 
 
 def call(kernel, out_shape, scratch, flops, args):
@@ -307,40 +282,42 @@
     )
     half_rows, half_cols = rows // 2, cols // 2
     shape = jax.ShapeDtypeStruct((1, half_rows, half_cols, wide), BF16)
-    field = call(
+    sides = 1 if strips == 2 else 2
+    field, ends = call(
         fine_rest_kernel,
-        shape,
+        (shape, jax.ShapeDtypeStruct((sides, half_cols, wide), BF16)),
         [pltpu.VMEM((rows + 1, cols + 8, channels), F32)],
         flops,
         (earlier, above_1, below_1, conv_fine, own, halo, conv_down),
     )
-    sides = 1 if strips == 2 else 2
+    field_2 = ring(field, 2)
+    if sides == 1:
+        rim = swapped(ends, 0)
+    else:
+        rim = jnp.concatenate([moved(ends[1:], 0, 1), moved(ends[:1], 0, -1)], axis=0)
+    rim_2 = ring(rim, 2)
     sums = jax.ShapeDtypeStruct((half_rows * half_cols, wide), F32)
-    rims = jax.ShapeDtypeStruct((sides, half_cols, wide), F32)
     flops = 2 * half_rows * half_cols * 9 * wide * wide
-    field_2 = ring(field, 2)
-    body, rim = call(coarse_first_kernel, (sums, rims), [], flops, (field, conv_coarse))
-    field_2, body, rim = lax.optimization_barrier((field_2, body, rim))
+    total = call(coarse_first_kernel, sums, [], flops, (field, rim, conv_coarse))
     if times % 2 == 0:
-        direct, relayed = paired(field), paired(field_2)
+        direct, direct_rim = paired(field), paired(rim)
     else:
-        direct = relayed = moved(field, 1, 0)
-    body, rim = call(
-        coarse_next_kernel, (sums, rims), [], flops, (field_2, conv_coarse, body, rim)
-    )
-    rim = call(
-        coarse_rim_kernel,
-        jax.ShapeDtypeStruct(rims.shape, BF16),
+        direct, direct_rim = ring(field, 1), ring(rim, 1)
+    field_2, rim_2, total, direct, direct_rim = lax.optimization_barrier(
+        (field_2, rim_2, total, direct, direct_rim)
+    )
+    if times % 2 == 0:
+        relayed, relayed_rim = paired(field_2), paired(rim_2)
+    else:
+        relayed, relayed_rim = direct, direct_rim
+    total = call(coarse_next_kernel, sums, [], flops, (field_2, rim_2, conv_coarse, total))
+    return call(
+        coarse_last_kernel,
+        shape,
         [],
-        flops // 4,
-        (direct, relayed, conv_coarse, rim),
-    )
-    if sides == 1:
-        from_above = from_below = swapped(rim, 0)
-    else:
-        from_above, from_below = moved(rim[1:], 0, 1), moved(rim[:1], 0, -1)
-    total = call(coarse_last_kernel, sums, [], flops, (direct, relayed, conv_coarse, body))
-    return call(finish_kernel, shape, [], sums.size, (total, from_above, from_below))
+        flops,
+        (direct, direct_rim, relayed, relayed_rim, conv_coarse, total),
+    )
 
 
 def solution(mesh):

time: 29 us -> 29.8 us (1.028)
  starting transfers between devices: 9.46 us -> 11 us
  waiting for transfers between devices: 12.2 us -> 11.6 us
    ppermute x2 -> x3, starting transfers between devices: 2.1 us -> 4.55 us  [ring(): return lax.ppermute(value, 'tm', [(t, (t + steps) % tm) for t in range(tm)])]
    ppermute x2 -> x3, waiting for transfers between devices: 9.19 us -> 7.24 us  [ring(): return lax.ppermute(value, 'tm', [(t, (t + steps) % tm) for t in range(tm)])]
    ppermute x3, waiting for transfers between devices: 2.13 us -> 3.98 us  [swapped(): return lax.ppermute(value, ('tm', 'rows'), pairs)]
    ppermute x3, starting transfers between devices: 7.36 us -> 5.88 us  [swapped(): return lax.ppermute(value, ('tm', 'rows'), pairs)]
    ppermute x2 -> x4, starting transfers between devices: 0.01 us -> 0.58 us  [paired(): lax.ppermute(value, 'tm', [(t, t ^ 1) for t in range(lax.axis_size('tm'))])]
    ppermute x2 -> x4, waiting for transfers between devices: 0.85 us -> 0.41 us  [paired(): lax.ppermute(value, 'tm', [(t, t ^ 1) for t in range(lax.axis_size('tm'))])]
    pallas_call x10 -> x8, Pallas kernels: 6.56 us -> 6.35 us  [call(): pl.pallas_call(kernel, out_shape=out_shape, in_specs=[pl.BlockSpec(memory...]
  transfers between devices with their start and end apart: 7 -> 10, of which waited for: 6 -> 6; matrix products, arithmetic and copies ran while one was open for 0% -> 0% of each run, Pallas kernels for 12% -> 10%
where the time goes in v5:
time: 29.8 us; the launch traced here: 29.6 us
  waiting for transfers between devices  11.6 us (39%)
  starting transfers between devices  11 us (37%)
  Pallas kernels  6.35 us (21%)
  local copies, waits for them, and re-layouts  0.56 us (2%)
    ppermute x3, waiting for transfers between devices, ring(): return lax.ppermute(value, 'tm', [(t, (t + steps) % tm) for t in range(tm)])  7.24 us
    pallas_call x8, Pallas kernels, call(): pl.pallas_call(kernel, out_shape=out_shape, in_specs=[pl.BlockSpec(memory...  6.35 us
    ppermute x3, starting transfers between devices, swapped(): return lax.ppermute(value, ('tm', 'rows'), pairs)  5.88 us
    ppermute x3, starting transfers between devices, ring(): return lax.ppermute(value, 'tm', [(t, (t + steps) % tm) for t in range(tm)])  4.55 us
    ppermute x3, waiting for transfers between devices, swapped(): return lax.ppermute(value, ('tm', 'rows'), pairs)  3.98 us
  transfers between devices with their start and end apart: 10, of which 6 were waited for; matrix products, arithmetic and copies ran while one was open for 0% of the time, Pallas kernels for 10%

profile of v5, /device:TPU:0, one launch (start us, length us, event | category | flops | bytes accessed | tf_op | source)
XLA Modules:
  0.0 29.6 jit_solution(11979071063870802743)
XLA Ops:
  0.0 0.0 copy-start.1
  0.0 0.0 copy-start.2
  0.0 0.5 %collective-permute-start = (bf16[2,8,128,128]{3,2,1,0:T(8,128)(2,1)}, bf16[2,8,128,128]{3,2,1,0:T(8,128)(2,1)S(1)}, u32[]{:S(2)}, u32[]{:S(2)}) collective-permute-start(bf16[2,8,128,128]{3,2,1,0:T(8,128)(2,1)} %frames.1), channel_id=1, source_target_pairs={{0,2},{2,4},{4,6},{6,8},{8,10},{10,12},{12,14},{14,16},{16,18},{18... | collective-permute-start | bytes 1572872 | tf_op jit(solution)/shard_map/ppermute | solution.py:27
  0.5 0.5 %copy-done.1 = bf16[2,8,128,128]{3,2,1,0:T(8,128)(2,1)S(1)} copy-done((bf16[2,8,128,128]{3,2,1,0:T(8,128)(2,1)S(1)}, bf16[2,8,128,128]{3,2,1,0:T(8,128)(2,1)}, u32[]{:S(2)}) %copy-start.1) | copy-done | bytes 524312
  1.0 0.0 copy-start.3
  1.1 3.1 %collective-permute-start.2 = (bf16[2,2,128,128]{3,2,1,0:T(8,128)(2,1)S(1)}, bf16[2,2,128,128]{3,2,1,0:T(8,128)(2,1)S(1)}, u32[]{:S(2)}, u32[]{:S(2)}) collective-permute-start(bf16[2,2,128,128]{3,2,1,0:T(8,128)(2,1)S(1)} %shard_map.47), channel_id=1, source_target_pairs={{0,1},{1,0},{2,3},{3,2},{4,5},{5,4},{6,7},{7,6},{8,9},{9,8},{10,11... | collective-permute-start | bytes 393224 | tf_op jit(solution)/shard_map/ppermute | solution.py:33
  4.1 2.3 %collective-permute-start.1 = (bf16[2,2,128,128]{3,2,1,0:T(8,128)(2,1)S(1)}, bf16[2,2,128,128]{3,2,1,0:T(8,128)(2,1)S(1)}, u32[]{:S(2)}, u32[]{:S(2)}) collective-permute-start(bf16[2,2,128,128]{3,2,1,0:T(8,128)(2,1)S(1)} %shard_map.47), channel_id=1, source_target_pairs={{0,3},{1,2},{2,5},{3,4},{4,7},{5,6},{6,9},{7,8},{8,11},{9,10},{10,... | collective-permute-start | bytes 393224 | tf_op jit(solution)/shard_map/ppermute | solution.py:33
  6.4 0.0 copy-done.2
  6.4 1.5 %shard_map.48.own = f32[1152,256]{1,0:T(8,128)S(1)} custom-call(bf16[2,8,128,128]{3,2,1,0:T(8,128)(2,1)S(1)} %copy-done.1, bf16[3,3,384,128]{3,2,1,0:T(8,128)(2,1)S(1)} %copy-done.2), custom_call_target="tpu_custom_call" | custom-call | flops 1358954496 | bytes 1409024 | tf_op jit(solution)/shard_map/pallas_call | solution.py:253
  8.0 0.0 copy-start
  8.0 0.4 %collective-permute-done.2.above.below = bf16[2,2,128,128]{3,2,1,0:T(8,128)(2,1)S(1)} collective-permute-done((bf16[2,2,128,128]{3,2,1,0:T(8,128)(2,1)S(1)}, bf16[2,2,128,128]{3,2,1,0:T(8,128)(2,1)S(1)}, u32[]{:S(2)}, u32[]{:S(2)}) %collective-permute-start.2) | collective-permute-done | bytes 131104 | tf_op jit(solution)/shard_map/ppermute | solution.py:33
  8.4 0.4 %shard_map.49.halo = f32[384,256]{1,0:T(8,128)S(1)} custom-call(bf16[2,2,128,128]{3,2,1,0:T(8,128)(2,1)S(1)} %collective-permute-done.2.above.below, bf16[2,2,128,128]{3,2,1,0:T(8,128)(2,1)S(1)} %collective-permute-done.2.above.below, bf16[3,3,384,128]{3,2,1,0:T(8,128)(2,1)S(1)} %copy-done.2), custom_call_target="tpu_custom_call" | custom-call | flops 452984832 | bytes 1146880 | tf_op jit(solution)/shard_map/pallas_call | solution.py:253
  8.8 0.2 collective-permute-done.1.above.below
  9.0 3.6 %collective-permute-done.frames = bf16[2,8,128,128]{3,2,1,0:T(8,128)(2,1)S(1)} collective-permute-done((bf16[2,8,128,128]{3,2,1,0:T(8,128)(2,1)}, bf16[2,8,128,128]{3,2,1,0:T(8,128)(2,1)S(1)}, u32[]{:S(2)}, u32[]{:S(2)}) %collective-permute-start) | collective-permute-done | bytes 524320 | tf_op jit(solution)/shard_map/ppermute | solution.py:27
  12.6 0.0 copy-done.3
  12.6 2.2 %shard_map.50 = (bf16[1,4,64,256]{3,2,1,0:T(8,128)(2,1)S(1)}, bf16[1,64,256]{2,1,0:T(8,128)(2,1)S(1)}) custom-call(bf16[2,8,128,128]{3,2,1,0:T(8,128)(2,1)S(1)} %collective-permute-done.frames, bf16[2,2,128,128]{3,2,1,0:T(8,128)(2,1)S(1)} %collective-permute-done.1.above.below, bf16[2,2,128,128]{3,2,1,0:T(8,128)(2,1)S(1)} %collective-permute-done.1.above.below, ...), custom_call_target="tpu_custom_call" | custom-call | flops 1358954496 | bytes 3833856 | tf_op jit(solution)/shard_map/pallas_call | solution.py:253
  14.9 0.1 collective-permute-start.6
  14.9 1.6 %collective-permute-start.3 = (bf16[1,4,64,256]{3,2,1,0:T(8,128)(2,1)S(1)}, bf16[1,4,64,256]{3,2,1,0:T(8,128)(2,1)S(1)}, u32[]{:S(2)}, u32[]{:S(2)}) collective-permute-start(bf16[1,4,64,256]{3,2,1,0:T(8,128)(2,1)S(1)} %get-tuple-element.12.field), channel_id=1, source_target_pairs={{0,4},{2,6},{4,8},{6,10},{8,12},{10,14},{12,16},{14,18},{16,20},{1... | collective-permute-start | bytes 393224 | tf_op jit(solution)/shard_map/ppermute | solution.py:27
  16.5 0.5 %collective-permute-start.4 = (bf16[1,64,256]{2,1,0:T(8,128)(2,1)S(1)}, bf16[1,64,256]{2,1,0:T(8,128)(2,1)S(1)}, u32[]{:S(2)}, u32[]{:S(2)}) collective-permute-start(bf16[1,64,256]{2,1,0:T(8,128)(2,1)S(1)} %get-tuple-element.13), channel_id=1, source_target_pairs={{0,1},{1,0},{2,3},{3,2},{4,5},{5,4},{6,7},{7,6},{8,9},{9,8},{10,11... | collective-permute-start | bytes 98312 | tf_op jit(solution)/shard_map/ppermute | solution.py:33
  17.1 3.4 %collective-permute-done.4.rim = bf16[1,64,256]{2,1,0:T(8,128)(2,1)S(1)} collective-permute-done((bf16[1,64,256]{2,1,0:T(8,128)(2,1)S(1)}, bf16[1,64,256]{2,1,0:T(8,128)(2,1)S(1)}, u32[]{:S(2)}, u32[]{:S(2)}) %collective-permute-start.4) | collective-permute-done | bytes 32800 | tf_op jit(solution)/shard_map/ppermute | solution.py:33
  20.5 0.0 collective-permute-start.7
  20.5 2.5 %collective-permute-start.5 = (bf16[1,64,256]{2,1,0:T(8,128)(2,1)S(1)}, bf16[1,64,256]{2,1,0:T(8,128)(2,1)S(1)}, u32[]{:S(2)}, u32[]{:S(2)}) collective-permute-start(bf16[1,64,256]{2,1,0:T(8,128)(2,1)S(1)} %collective-permute-done.4.rim), channel_id=1, source_target_pairs={{0,4},{2,6},{4,8},{6,10},{8,12},{10,14},{12,16},{14,18},{16,20},{1... | collective-permute-start | bytes 98312 | tf_op jit(solution)/shard_map/ppermute | solution.py:27
  22.9 0.0 copy-done
  22.9 0.5 %shard_map.51.total = f32[256,256]{1,0:T(8,128)S(1)} custom-call(bf16[1,4,64,256]{3,2,1,0:T(8,128)(2,1)S(1)} %get-tuple-element.12.field, bf16[1,64,256]{2,1,0:T(8,128)(2,1)S(1)} %collective-permute-done.4.rim, bf16[3,3,768,256]{3,2,1,0:T(8,128)(2,1)S(1)} %copy-done), custom_call_target="tpu_custom_call" | custom-call | flops 301989888 | bytes 3702784 | tf_op jit(solution)/shard_map/pallas_call | solution.py:253
  23.4 0.0 collective-permute-done.7.direct_rim
  23.4 3.7 %collective-permute-done.5.rim = bf16[1,64,256]{2,1,0:T(8,128)(2,1)S(1)} collective-permute-done((bf16[1,64,256]{2,1,0:T(8,128)(2,1)S(1)}, bf16[1,64,256]{2,1,0:T(8,128)(2,1)S(1)}, u32[]{:S(2)}, u32[]{:S(2)}) %collective-permute-start.5) | collective-permute-done | bytes 32800 | tf_op jit(solution)/shard_map/ppermute | solution.py:27
  27.1 0.0 collective-permute-done.6.direct
  27.1 0.0 collective-permute-done.3.field
  27.1 0.0 collective-permute-start.8
  27.1 0.5 %collective-permute-start.9 = (bf16[1,64,256]{2,1,0:T(8,128)(2,1)S(1)}, bf16[1,64,256]{2,1,0:T(8,128)(2,1)S(1)}, u32[]{:S(2)}, u32[]{:S(2)}) collective-permute-start(bf16[1,64,256]{2,1,0:T(8,128)(2,1)S(1)} %collective-permute-done.5.rim), channel_id=1, source_target_pairs={{0,2},{2,0},{4,6},{6,4},{8,10},{10,8},{12,14},{14,12},{16,18},{18,... | collective-permute-start | bytes 98312 | tf_op jit(solution)/shard_map/ppermute | solution.py:37
  27.6 0.5 %shard_map.52.total = f32[256,256]{1,0:T(8,128)S(1)} custom-call(bf16[1,4,64,256]{3,2,1,0:T(8,128)(2,1)S(1)} %collective-permute-done.3.field, bf16[1,64,256]{2,1,0:T(8,128)(2,1)S(1)} %collective-permute-done.5.rim, bf16[3,3,768,256]{3,2,1,0:T(8,128)(2,1)S(1)} %copy-done, f32[256,256]{1,0:T(8,128)S(1)} %shard_map.51.total), custom_call_target="tpu_custom_call" | custom-call | flops 301989888 | bytes 3964928 | tf_op jit(solution)/shard_map/pallas_call | solution.py:253
  28.1 0.4 %collective-permute-done.9.relayed_rim = bf16[1,64,256]{2,1,0:T(8,128)(2,1)S(1)} collective-permute-done((bf16[1,64,256]{2,1,0:T(8,128)(2,1)S(1)}, bf16[1,64,256]{2,1,0:T(8,128)(2,1)S(1)}, u32[]{:S(2)}, u32[]{:S(2)}) %collective-permute-start.9) | collective-permute-done | bytes 32800 | tf_op jit(solution)/shard_map/ppermute | solution.py:37
  28.5 0.0 collective-permute-done.8.relayed
  28.5 1.2 %shard_map.53 = bf16[1,4,64,256]{3,2,1,0:T(8,128)(2,1)} custom-call(bf16[1,4,64,256]{3,2,1,0:T(8,128)(2,1)S(1)} %collective-permute-done.6.direct, bf16[1,64,256]{2,1,0:T(8,128)(2,1)S(1)} %collective-permute-done.7.direct_rim, bf16[1,4,64,256]{3,2,1,0:T(8,128)(2,1)S(1)} %collective-permute-done.8.relayed, ...), custom_call_target="tpu_custom_call" | custom-call | flops 301989888 | bytes 4128768 | tf_op jit(solution)/shard_map/pallas_call | solution.py:253
  (2 shorter events, 0.0 us)
Async XLA Ops:
  0.0 1.0 %copy-start.1 = (bf16[2,8,128,128]{3,2,1,0:T(8,128)(2,1)S(1)}, bf16[2,8,128,128]{3,2,1,0:T(8,128)(2,1)}, u32[]{:S(2)}) copy-start(bf16[2,8,128,128]{3,2,1,0:T(8,128)(2,1)} %frames.1) | copy-start | bytes 1572868
  0.0 6.4 %copy-start.2 = (bf16[3,3,384,128]{3,2,1,0:T(8,128)(2,1)S(1)}, bf16[3,3,384,128]{3,2,1,0:T(8,128)(2,1)}, u32[]{:S(2)}) copy-start(bf16[3,3,384,128]{3,2,1,0:T(8,128)(2,1)} %weight.8) | copy-start | bytes 2654212
  0.0 12.6 %collective-permute-start = (bf16[2,8,128,128]{3,2,1,0:T(8,128)(2,1)}, bf16[2,8,128,128]{3,2,1,0:T(8,128)(2,1)S(1)}, u32[]{:S(2)}, u32[]{:S(2)}) collective-permute-start(bf16[2,8,128,128]{3,2,1,0:T(8,128)(2,1)} %frames.1), channel_id=1, source_target_pairs={{0,2},{2,4},{4,6},{6,8},{8,10},{10,12},{12,14},{14,16},{16,18},{18... | collective-permute-start | bytes 1572872 | tf_op jit(solution)/shard_map/ppermute | solution.py:27
  1.0 11.6 %copy-start.3 = (bf16[3,384,256]{2,1,0:T(8,128)(2,1)S(1)}, bf16[3,384,256]{2,1,0:T(8,128)(2,1)}, u32[]{:S(2)}) copy-start(bf16[3,384,256]{2,1,0:T(8,128)(2,1)} %down.1) | copy-start | bytes 1769476
  1.1 7.3 %collective-permute-start.2 = (bf16[2,2,128,128]{3,2,1,0:T(8,128)(2,1)S(1)}, bf16[2,2,128,128]{3,2,1,0:T(8,128)(2,1)S(1)}, u32[]{:S(2)}, u32[]{:S(2)}) collective-permute-start(bf16[2,2,128,128]{3,2,1,0:T(8,128)(2,1)S(1)} %shard_map.47), channel_id=1, source_target_pairs={{0,1},{1,0},{2,3},{3,2},{4,5},{5,4},{6,7},{7,6},{8,9},{9,8},{10,11... | collective-permute-start | bytes 393224 | tf_op jit(solution)/shard_map/ppermute | solution.py:33
  4.1 4.9 %collective-permute-start.1 = (bf16[2,2,128,128]{3,2,1,0:T(8,128)(2,1)S(1)}, bf16[2,2,128,128]{3,2,1,0:T(8,128)(2,1)S(1)}, u32[]{:S(2)}, u32[]{:S(2)}) collective-permute-start(bf16[2,2,128,128]{3,2,1,0:T(8,128)(2,1)S(1)} %shard_map.47), channel_id=1, source_target_pairs={{0,3},{1,2},{2,5},{3,4},{4,7},{5,6},{6,9},{7,8},{8,11},{9,10},{10,... | collective-permute-start | bytes 393224 | tf_op jit(solution)/shard_map/ppermute | solution.py:33
  8.0 14.9 %copy-start = (bf16[3,3,768,256]{3,2,1,0:T(8,128)(2,1)S(1)}, bf16[3,3,768,256]{3,2,1,0:T(8,128)(2,1)}, u32[]{:S(2)}) copy-start(bf16[3,3,768,256]{3,2,1,0:T(8,128)(2,1)} %weight.11) | copy-start | bytes 10616836
  14.9 12.2 %collective-permute-start.6 = (bf16[1,4,64,256]{3,2,1,0:T(8,128)(2,1)S(1)}, bf16[1,4,64,256]{3,2,1,0:T(8,128)(2,1)S(1)}, u32[]{:S(2)}, u32[]{:S(2)}) collective-permute-start(bf16[1,4,64,256]{3,2,1,0:T(8,128)(2,1)S(1)} %get-tuple-element.12.field), channel_id=1, source_target_pairs={{0,2},{2,0},{4,6},{6,4},{8,10},{10,8},{12,14},{14,12},{16,18},{18,... | collective-permute-start | bytes 393224 | tf_op jit(solution)/shard_map/ppermute | solution.py:37
  14.9 12.1 %collective-permute-start.3 = (bf16[1,4,64,256]{3,2,1,0:T(8,128)(2,1)S(1)}, bf16[1,4,64,256]{3,2,1,0:T(8,128)(2,1)S(1)}, u32[]{:S(2)}, u32[]{:S(2)}) collective-permute-start(bf16[1,4,64,256]{3,2,1,0:T(8,128)(2,1)S(1)} %get-tuple-element.12.field), channel_id=1, source_target_pairs={{0,4},{2,6},{4,8},{6,10},{8,12},{10,14},{12,16},{14,18},{16,20},{1... | collective-permute-start | bytes 393224 | tf_op jit(solution)/shard_map/ppermute | solution.py:27
  16.5 3.9 %collective-permute-start.4 = (bf16[1,64,256]{2,1,0:T(8,128)(2,1)S(1)}, bf16[1,64,256]{2,1,0:T(8,128)(2,1)S(1)}, u32[]{:S(2)}, u32[]{:S(2)}) collective-permute-start(bf16[1,64,256]{2,1,0:T(8,128)(2,1)S(1)} %get-tuple-element.13), channel_id=1, source_target_pairs={{0,1},{1,0},{2,3},{3,2},{4,5},{5,4},{6,7},{7,6},{8,9},{9,8},{10,11... | collective-permute-start | bytes 98312 | tf_op jit(solution)/shard_map/ppermute | solution.py:33
  20.5 2.9 %collective-permute-start.7 = (bf16[1,64,256]{2,1,0:T(8,128)(2,1)S(1)}, bf16[1,64,256]{2,1,0:T(8,128)(2,1)S(1)}, u32[]{:S(2)}, u32[]{:S(2)}) collective-permute-start(bf16[1,64,256]{2,1,0:T(8,128)(2,1)S(1)} %collective-permute-done.4.rim), channel_id=1, source_target_pairs={{0,2},{2,0},{4,6},{6,4},{8,10},{10,8},{12,14},{14,12},{16,18},{18,... | collective-permute-start | bytes 98312 | tf_op jit(solution)/shard_map/ppermute | solution.py:37
  20.5 6.6 %collective-permute-start.5 = (bf16[1,64,256]{2,1,0:T(8,128)(2,1)S(1)}, bf16[1,64,256]{2,1,0:T(8,128)(2,1)S(1)}, u32[]{:S(2)}, u32[]{:S(2)}) collective-permute-start(bf16[1,64,256]{2,1,0:T(8,128)(2,1)S(1)} %collective-permute-done.4.rim), channel_id=1, source_target_pairs={{0,4},{2,6},{4,8},{6,10},{8,12},{10,14},{12,16},{14,18},{16,20},{1... | collective-permute-start | bytes 98312 | tf_op jit(solution)/shard_map/ppermute | solution.py:27
  27.1 1.4 %collective-permute-start.8 = (bf16[1,4,64,256]{3,2,1,0:T(8,128)(2,1)S(1)}, bf16[1,4,64,256]{3,2,1,0:T(8,128)(2,1)S(1)}, u32[]{:S(2)}, u32[]{:S(2)}) collective-permute-start(bf16[1,4,64,256]{3,2,1,0:T(8,128)(2,1)S(1)} %collective-permute-done.3.field), channel_id=1, source_target_pairs={{0,2},{2,0},{4,6},{6,4},{8,10},{10,8},{12,14},{14,12},{16,18},{18,... | collective-permute-start | bytes 393224 | tf_op jit(solution)/shard_map/ppermute | solution.py:37
  27.1 1.4 %collective-permute-start.9 = (bf16[1,64,256]{2,1,0:T(8,128)(2,1)S(1)}, bf16[1,64,256]{2,1,0:T(8,128)(2,1)S(1)}, u32[]{:S(2)}, u32[]{:S(2)}) collective-permute-start(bf16[1,64,256]{2,1,0:T(8,128)(2,1)S(1)} %collective-permute-done.5.rim), channel_id=1, source_target_pairs={{0,2},{2,0},{4,6},{6,4},{8,10},{10,8},{12,14},{14,12},{16,18},{18,... | collective-permute-start | bytes 98312 | tf_op jit(solution)/shard_map/ppermute | solution.py:37
